TPU v7x, 256 devices: a whole 4x4x8 slice. The times are simulated.
256 devices in a mesh: grp: 16 (over x, y), tile: 16 (over z, core).
Axes of the slice: x: 4, y: 4, z: 8, core: 2. Of those that a mesh axis runs over, the one named last changes fastest.
Arguments:
- starting_realizations: float32 [1024, 2, 4, 128, 128], P('grp', None, None, 'tile'), may hold values from -6 to 6
- diffusivity: float32 [4, 128], replicated, may hold values from 0.1 to 0.24
- eastward_velocity: float32 [4], replicated, may hold values from -0.4 to 0.4
- northward_velocity: float32 [4], replicated, may hold values from -0.4 to 0.4
- obs_cell: int32 [16, 16, 256], P('tile'), may hold values from 0 to 2047
- obs_count: int32 [16, 16], P('tile', 'grp'), may hold values from 1 to 256
- obs_value: float32 [16, 16, 256], P('tile', 'grp'), may hold values from -15 to 15
- obs_weight: float32 [16, 16, 256], P('tile', 'grp'), may hold values from 0.05 to 0.5
Outputs:
- analysis: bfloat16 [1024, 2, 4, 128, 128], P('grp', None, None, 'tile')
All inputs are finite; a program needn't handle non-finite values.
Results may differ from a plain program's by a relative error of at most 0.0062.
Values may be sent and summed in bfloat16 or wider, within the bound.
A program may use at most 128 MiB of HBM per device.

v0:
```python
import jax
import jax.numpy as jnp
from jax import lax
from jax.experimental import pallas as pl
from jax.experimental.pallas import tpu as pltpu
from jax.sharding import PartitionSpec as P


F32 = jnp.float32
BF16 = jnp.bfloat16
HIGH = lax.Precision.HIGHEST
VMEM = pl.BlockSpec(memory_space=pltpu.VMEM)
SMEM = pl.BlockSpec(memory_space=pltpu.SMEM)
MEMBERS = 1024.0
PARAMS = pltpu.CompilerParams(vmem_limit_bytes=48 * 1024 * 1024)


def nt(a, b, precision=None):
    return lax.dot_general(a, b, (((1,), (1,)), ((), ())), precision=precision, preferred_element_type=F32)


def nn(a, b, precision=None):
    return lax.dot_general(a, b, (((1,), (0,)), ((), ())), precision=precision, preferred_element_type=F32)


def turn_in(x_ref, z_ref, low_ref, high_ref):
    for row in range(8):
        for level in range(4):
            start = level * 8 + row
            plane = jnp.concatenate(
                [x_ref[pl.ds(start, 64, stride=64), :], x_ref[pl.ds(start + 32, 64, stride=64), :]], axis=0
            )
            z_ref[pl.ds((row // 2) * 1024 + (row % 2) * 4 + level, 128, stride=8), :] = plane.T
    low_ref[...] = z_ref[0:1024, :].astype(BF16)
    high_ref[...] = z_ref[3072:4096, :].astype(BF16)


def stencil(v_ref, k_list, y0, count, coef, sub):
    d, u, v = coef
    east_c, west_c, north_c, south_c = d - u, d + u, d - v, d + v
    mid_c = 1.0 - 4.0 * d
    upper = sub < 4
    centers = {}
    rolled = {}
    for k in range(6):
        centers[k] = v_ref[k, pl.ds(y0 + 1, count)]
        rolled[k] = pltpu.roll(centers[k], 4, 1)
    outs = []
    for k in k_list:
        east = jnp.where(upper, rolled[k], rolled[k + 1]) if k < 5 else rolled[k]
        west = jnp.where(upper, rolled[k - 1], rolled[k]) if k > 0 else rolled[k]
        north = v_ref[k, pl.ds(y0 + 2, count)]
        south = v_ref[k, pl.ds(y0, count)]
        outs.append(centers[k] * mid_c + east * east_c + west * west_c + north * north_c + south * south_c)
    return outs


def wrap(v_ref):
    for k in range(6):
        v_ref[k, 0] = v_ref[k, 128]
        v_ref[k, 129] = v_ref[k, 1]


def forecast(z_ref, low_ref, high_ref, d_ref, u_ref, v_ref, s_ref, down_ref, up_ref, first, second):
    first[0, 1:129] = low_ref[...].astype(F32).reshape(128, 8, 128)
    first[5, 1:129] = high_ref[...].astype(F32).reshape(128, 8, 128)
    for k in range(4):
        first[k + 1, 1:129] = z_ref[k * 1024:(k + 1) * 1024, :].reshape(128, 8, 128)
    wrap(first)
    sub = lax.broadcasted_iota(jnp.int32, (8, 8, 128), 1)
    u = 0.5 * u_ref[...][None]
    v = 0.5 * v_ref[...][None]

    @pl.loop(0, 16)
    def _(step):
        y0 = step * 8
        coef = (d_ref[pl.ds(y0, 8)], u, v)
        for k, value in enumerate(stencil(first, range(6), y0, 8, coef, sub)):
            second[k, pl.ds(y0 + 1, 8)] = value

    wrap(second)

    @pl.loop(0, 16)
    def _(step):
        y0 = step * 8
        coef = (d_ref[pl.ds(y0, 8)], u, v)
        for k, value in enumerate(stencil(second, range(1, 5), y0, 8, coef, sub)):
            packed = value.reshape(64, 128).astype(BF16)
            s_ref[step, k * 64:(k + 1) * 64, :] = packed
            if k < 2:
                down_ref[step, k * 64:(k + 1) * 64, :] = packed
            else:
                up_ref[step, (k - 2) * 64:(k - 1) * 64, :] = packed


def observe(s_ref, low_ref, high_ref, cell_ref, ob_ref):
    cell = cell_ref[...]
    level_index = cell // 256
    rest = cell % 256
    row = rest // 16
    col = rest % 16
    half = (level_index // 4)
    index = (row // 2) * 128 + col * 8 + (row % 2) * 4 + level_index % 4
    lane = lax.broadcasted_iota(jnp.int32, (256, 128), 1)
    left = lane < 64
    left_half = left[0:128]
    for b in range(16):
        before, after = (b + 15) % 16, (b + 1) % 16
        index_b = index[:, b:b + 1]
        half_b = half[:, b:b + 1]
        picks, pieces = [], []
        for kk in range(8):
            picks.append(jnp.where(index_b == lane + kk * 128, 1.0, 0.0).astype(BF16))
            if kk < 2:
                source, k = low_ref, kk
            elif kk < 6:
                source, k = s_ref, kk - 2
            else:
                source, k = high_ref, kk - 6
            pieces.append(source[before, k * 64 + 32:k * 64 + 64, :])
            pieces.append(source[b, k * 64:k * 64 + 64, :])
            pieces.append(source[after, k * 64:k * 64 + 32, :])
        values = nn(jnp.concatenate(picks, axis=1), jnp.concatenate(pieces, axis=0))
        values = jnp.where((half_b == 0) == left, values, 0.0)
        values = values + pltpu.roll(values, 64, 1)
        ob_ref[b] = jnp.where(left_half, values[0:128], values[128:256]).astype(BF16)


def solve(ob_ref, s_ref, weight_ref, value_ref, count_ref, out_ref, basis, dev_all):
    lane = lax.broadcasted_iota(jnp.int32, (128, 128), 1)
    left = lane < 64
    left2 = lax.broadcasted_iota(jnp.int32, (256, 128), 1) < 64
    total = ob_ref[0].astype(F32)
    for g in range(1, 16):
        total = total + ob_ref[g].astype(F32)
    mean0 = jnp.sum(jnp.where(left, total, 0.0), axis=1, keepdims=True) * (1.0 / MEMBERS)
    mean1 = jnp.sum(jnp.where(left, 0.0, total), axis=1, keepdims=True) * (1.0 / MEMBERS)
    count = count_ref[0, 0]
    row_lane = lax.broadcasted_iota(jnp.int32, (1, 128), 1)
    root0 = jnp.sqrt(jnp.where(row_lane < count, weight_ref[0:1, :], 0.0))
    root1 = jnp.sqrt(jnp.where(row_lane + 128 < count, weight_ref[1:2, :], 0.0))
    root0 = jnp.broadcast_to(root0, (128, 128)).T
    root1 = jnp.broadcast_to(root1, (128, 128)).T
    target0 = jnp.broadcast_to(value_ref[0:1, :], (128, 128)).T
    target1 = jnp.broadcast_to(value_ref[1:2, :], (128, 128)).T
    misfit = jnp.concatenate([root0 * (target0 - mean0), root1 * (target1 - mean1)], axis=0)
    mean = jnp.where(left, mean0, mean1)
    root = jnp.where(left, root0, root1)
    zero = jnp.zeros((256, 128), BF16)
    for g in range(16):
        scaled = (ob_ref[g].astype(F32) - mean) * root
        turned = pltpu.roll(scaled, 64, 1)
        both = jnp.concatenate(
            [jnp.where(left, scaled, turned), jnp.where(left, turned, scaled)], axis=0
        )
        basis[0:256, g * 128:(g + 1) * 128] = jnp.where(left2, both, 0.0).astype(BF16)
        basis[256:512, g * 128:(g + 1) * 128] = jnp.where(left2, 0.0, both).astype(BF16)
    small = nt(basis[0:256, :], basis[0:256, :])
    eye = lax.broadcasted_iota(jnp.int32, (256, 256), 0) == lax.broadcasted_iota(jnp.int32, (256, 256), 1)
    trace = jnp.sum(jnp.where(eye, small, 0.0), axis=(0, 1), keepdims=True)
    s = (MEMBERS - 1.0) + trace * (1.0 / MEMBERS)
    inv_s = 1.0 / s
    inv_root_s = lax.rsqrt(s)
    a = (MEMBERS - 1.0) * inv_s
    p = 1.5 - 0.5 * a
    r0 = 1.5 * p - 0.5 * a * p * p * p
    r1 = -0.75 - 0.5 * p * p * p + 0.75 * a * p * p
    r2 = 0.5 * (1.5 * p * p - 0.75 * a * p)
    r3 = (1.0 / 6.0) * (0.375 * a - 2.25 * p)
    r4 = 1.5 / 24.0
    g1 = small * inv_s
    g2 = nn(g1, g1, HIGH)
    q = jnp.where(eye, r1, 0.0) + r2 * g1 + r3 * g2 + r4 * nn(g2, g1, HIGH)
    first = (r0 * misfit + nn(g1, nn(q, misfit, HIGH), HIGH)) * inv_root_s
    gain = (r0 * first + nn(g1, nn(q, first, HIGH), HIGH)) * inv_root_s
    spread = jnp.sqrt(jnp.full((1, 1), MEMBERS - 1.0, F32))
    mix = q * (spread * inv_s * inv_root_s)
    keep = r0 * spread * inv_root_s

    state_total = s_ref[0].astype(F32)
    for g in range(1, 16):
        state_total = state_total + s_ref[g].astype(F32)
    centre0 = jnp.sum(jnp.where(left2, state_total, 0.0), axis=1, keepdims=True) * (1.0 / MEMBERS)
    centre1 = jnp.sum(jnp.where(left2, 0.0, state_total), axis=1, keepdims=True) * (1.0 / MEMBERS)
    centre = jnp.where(left2, centre0, centre1)
    for g in range(16):
        dev_all[:, g * 128:(g + 1) * 128] = (s_ref[g].astype(F32) - centre).astype(BF16)
    cross = nt(dev_all[...], basis[...])
    cross0, cross1 = cross[:, 0:256], cross[:, 256:512]
    update = jnp.concatenate([nn(cross0, mix, HIGH), nn(cross1, mix, HIGH)], axis=1).astype(BF16)
    offset = centre + jnp.where(left2, nn(cross0, gain, HIGH), nn(cross1, gain, HIGH))
    for g in range(16):
        lanes = slice(g * 128, (g + 1) * 128)
        out_ref[g] = (offset + keep * dev_all[:, lanes].astype(F32) + nn(update, basis[:, lanes])).astype(BF16)


def turn_out(r_ref, out_ref, field, stage):
    for b in range(16):
        for k in range(4):
            field[pl.ds(k * 1024 + b * 64, 64), :] = r_ref[b, k * 64:(k + 1) * 64, :].astype(F32)
    for row in range(8):
        for level in range(4):
            start = level * 8 + row
            plane = field[pl.ds((row // 2) * 1024 + (row % 2) * 4 + level, 128, stride=8), :].T
            stage[pl.ds(start, 64, stride=64), :] = plane[0:64]
            stage[pl.ds(start + 32, 64, stride=64), :] = plane[64:128]
    out_ref[...] = stage[...].astype(BF16)


def call_turn_in(x):
    return pl.pallas_call(
        turn_in,
        out_shape=(
            jax.ShapeDtypeStruct((4096, 128), F32),
            jax.ShapeDtypeStruct((1024, 128), BF16),
            jax.ShapeDtypeStruct((1024, 128), BF16),
        ),
        in_specs=[VMEM],
        out_specs=(VMEM, VMEM, VMEM),
        compiler_params=PARAMS,
        name="turn_in",
    )(x)


def call_forecast(z, low, high, d, u, v):
    return pl.pallas_call(
        forecast,
        out_shape=(
            jax.ShapeDtypeStruct((16, 256, 128), BF16),
            jax.ShapeDtypeStruct((16, 128, 128), BF16),
            jax.ShapeDtypeStruct((16, 128, 128), BF16),
        ),
        in_specs=[VMEM] * 6,
        out_specs=(VMEM, VMEM, VMEM),
        scratch_shapes=[pltpu.VMEM((6, 130, 8, 128), F32), pltpu.VMEM((6, 130, 8, 128), F32)],
        compiler_params=PARAMS,
        name="forecast",
    )(z, low, high, d, u, v)


def call_observe(s, low, high, cell):
    return pl.pallas_call(
        observe,
        out_shape=jax.ShapeDtypeStruct((16, 128, 128), BF16),
        in_specs=[VMEM] * 4,
        out_specs=VMEM,
        compiler_params=PARAMS,
        name="observe",
    )(s, low, high, cell)


def call_solve(ob, s, weight, value, count):
    return pl.pallas_call(
        solve,
        out_shape=jax.ShapeDtypeStruct((16, 256, 128), BF16),
        in_specs=[VMEM, VMEM, VMEM, VMEM, SMEM],
        out_specs=VMEM,
        scratch_shapes=[pltpu.VMEM((512, 2048), BF16), pltpu.VMEM((256, 2048), BF16)],
        compiler_params=PARAMS,
        name="solve",
    )(ob, s, weight, value, count)


def call_turn_out(r):
    return pl.pallas_call(
        turn_out,
        out_shape=jax.ShapeDtypeStruct((4096, 128), BF16),
        in_specs=[VMEM],
        out_specs=VMEM,
        scratch_shapes=[pltpu.VMEM((4096, 128), F32), pltpu.VMEM((4096, 128), F32)],
        compiler_params=PARAMS,
        name="turn_out",
    )(r)


def coefficients(diffusivity, eastward_velocity, northward_velocity):
    d = jnp.broadcast_to(jnp.concatenate([diffusivity, diffusivity], 0).T[:, :, None], (128, 8, 128))
    u = jnp.broadcast_to(jnp.concatenate([eastward_velocity] * 2)[:, None], (8, 128))
    v = jnp.broadcast_to(jnp.concatenate([northward_velocity] * 2)[:, None], (8, 128))
    return d, u, v


def exchange(values):
    return lax.all_to_all(values, "grp", split_axis=0, concat_axis=0, tiled=True)


def on_device(
    starting_realizations,
    diffusivity,
    eastward_velocity,
    northward_velocity,
    obs_cell,
    obs_count,
    obs_value,
    obs_weight,
):
    count = lax.axis_size("tile")
    forward = [(i, (i + 1) % count) for i in range(count)]
    backward = [((i + 1) % count, i) for i in range(count)]
    d, u, v = coefficients(diffusivity, eastward_velocity, northward_velocity)
    z, bottom, top = call_turn_in(starting_realizations.reshape(4096, 128))
    low = lax.ppermute(top, "tile", forward)
    high = lax.ppermute(bottom, "tile", backward)
    states, down, up = call_forecast(z, low, high, d, u, v)
    low = lax.ppermute(up, "tile", forward)
    high = lax.ppermute(down, "tile", backward)
    blocked = exchange(states)
    measured = exchange(call_observe(states, low, high, obs_cell[0].T))
    updated = call_solve(
        measured, blocked, obs_weight.reshape(2, 128), obs_value.reshape(2, 128), obs_count
    )
    return call_turn_out(exchange(updated)).reshape(64, 2, 4, 8, 128)


def solution(mesh):
    return jax.shard_map(
        on_device,
        mesh=mesh,
        in_specs=(
            P("grp", None, None, "tile", None),
            P(),
            P(),
            P(),
            P("tile", None, None),
            P("tile", "grp"),
            P("tile", "grp", None),
            P("tile", "grp", None),
        ),
        out_specs=P("grp", None, None, "tile", None),
        check_vma=False,
    )
```

profile of v0, /device:TPU:97, one launch (start us, length us, event | category | flops | bytes accessed | tf_op | source)
XLA Modules:
  0.0 85.2 jit_solution(13148623329189002518)
XLA Ops:
  0.0 1.6 %copy-done = f32[64,2,4,8,128]{4,3,2,1,0:T(8,128)S(1)} copy-done((f32[64,2,4,8,128]{4,3,2,1,0:T(8,128)S(1)}, f32[64,2,4,8,128]{4,3,2,1,0:T(8,128)}, u32[]{:S(2)}) %copy-start) | copy-done | bytes 2097176
  1.6 1.4 %turn_in.1 = (f32[4096,128]{1,0:T(8,128)S(1)}, bf16[1024,128]{1,0:T(8,128)(2,1)S(1)}, bf16[1024,128]{1,0:T(8,128)(2,1)S(1)}) custom-call(f32[4096,128]{1,0:T(8,128)S(1)} %bitcast.9), custom_call_target="tpu_custom_call" | custom-call | tf_op jit(solution)/shard_map/turn_in/pallas_call | solution.py:211
  3.1 3.4 %collective-permute-start = (bf16[1024,128]{1,0:T(8,128)(2,1)S(1)}, bf16[1024,128]{1,0:T(8,128)(2,1)S(1)}, u32[]{:S(2)}, u32[]{:S(2)}) collective-permute-start(bf16[1024,128]{1,0:T(8,128)(2,1)S(1)} %get-tuple-element.12), channel_id=1, source_target_pairs={{0,1},{1,2},{2,3},{3,4},{4,5},{5,6},{6,7},{7,8},{8,9},{9,10},{10,1... | collective-permute-start | bytes 786440 | tf_op jit(solution)/shard_map/ppermute | solution.py:302
  6.5 0.1 copy.9
  6.6 0.1 pad_maximum_fusion
  6.7 0.1 pad_maximum_fusion.1
  6.8 3.0 %collective-permute-done.low_ref = bf16[1024,128]{1,0:T(8,128)(2,1)S(1)} collective-permute-done((bf16[1024,128]{1,0:T(8,128)(2,1)S(1)}, bf16[1024,128]{1,0:T(8,128)(2,1)S(1)}, u32[]{:S(2)}, u32[]{:S(2)}) %collective-permute-start) | collective-permute-done | bytes 262176 | tf_op jit(solution)/shard_map/ppermute | solution.py:302
  9.8 3.7 %collective-permute-done.1.high_ref = bf16[1024,128]{1,0:T(8,128)(2,1)S(1)} collective-permute-done((bf16[1024,128]{1,0:T(8,128)(2,1)S(1)}, bf16[1024,128]{1,0:T(8,128)(2,1)S(1)}, u32[]{:S(2)}, u32[]{:S(2)}) %collective-permute-start.1) | collective-permute-done | bytes 262176 | tf_op jit(solution)/shard_map/ppermute | solution.py:303
  13.5 0.2 broadcast_in_dim.6.d_ref
  13.7 0.1 broadcast_in_dim.7.u_ref
  13.8 0.1 broadcast_in_dim.8.v_ref
  13.8 4.0 %forecast.1 = (bf16[16,256,128]{2,1,0:T(8,128)(2,1)}, bf16[16,128,128]{2,1,0:T(8,128)(2,1)S(1)}, bf16[16,128,128]{2,1,0:T(8,128)(2,1)}) custom-call(f32[4096,128]{1,0:T(8,128)S(1)} %get-tuple-element.11.z_ref, bf16[1024,128]{1,0:T(8,128)(2,1)S(1)} %collective-permute-done.low_ref, bf16[1024,128]{1,0:T(8,128)(2,1)S(1)} %collective-permute-done.1.high_ref, ...), custom_call_target="tpu_custom_call" | custom-call | tf_op jit(solution)/shard_map/forecast/pallas_call | solution.py:226
  17.8 6.8 %all-to-all-start.1 = ((bf16[16,256,128]{2,1,0:T(8,128)(2,1)}), bf16[16,256,128]{2,1,0:T(8,128)(2,1)S(1)}, u32[]{:S(2)}, u32[]{:S(2)}) async-start(bf16[16,256,128]{2,1,0:T(8,128)(2,1)} %get-tuple-element.14.s_ref), calls=%async_computation.1 | async-start | bytes 2097152 | tf_op jit(solution)/shard_map/all_to_all | solution.py:284
  24.6 0.3 collective-permute-start.2
  24.9 0.2 collective-permute-start.3
  25.1 0.1 copy.10
  25.2 6.1 %collective-permute-done.2.low_ref = bf16[16,128,128]{2,1,0:T(8,128)(2,1)S(1)} collective-permute-done((bf16[16,128,128]{2,1,0:T(8,128)(2,1)}, bf16[16,128,128]{2,1,0:T(8,128)(2,1)S(1)}, u32[]{:S(2)}, u32[]{:S(2)}) %collective-permute-start.2) | collective-permute-done | bytes 524320 | tf_op jit(solution)/shard_map/ppermute | solution.py:305
  31.4 3.7 %collective-permute-done.3.high_ref = bf16[16,128,128]{2,1,0:T(8,128)(2,1)S(1)} collective-permute-done((bf16[16,128,128]{2,1,0:T(8,128)(2,1)S(1)}, bf16[16,128,128]{2,1,0:T(8,128)(2,1)S(1)}, u32[]{:S(2)}, u32[]{:S(2)}) %collective-permute-start.3) | collective-permute-done | bytes 524320 | tf_op jit(solution)/shard_map/ppermute | solution.py:306
  35.0 5.0 %observe.1 = bf16[16,128,128]{2,1,0:T(8,128)(2,1)} custom-call(bf16[16,256,128]{2,1,0:T(8,128)(2,1)} %get-tuple-element.14.s_ref, bf16[16,128,128]{2,1,0:T(8,128)(2,1)S(1)} %collective-permute-done.2.low_ref, bf16[16,128,128]{2,1,0:T(8,128)(2,1)S(1)} %collective-permute-done.3.high_ref, s32[256,16]{1,0:T(8,128)S(1)} %bitcast.10), custom_call_target="tpu_custom_call" | custom-call | tf_op jit(solution)/shard_map/observe/pallas_call | solution.py:242
  40.0 6.7 %all-to-all-start = ((bf16[16,128,128]{2,1,0:T(8,128)(2,1)}), bf16[16,128,128]{2,1,0:T(8,128)(2,1)S(1)}, u32[]{:S(2)}, u32[]{:S(2)}) async-start(bf16[16,128,128]{2,1,0:T(8,128)(2,1)} %observe.1), calls=%async_computation | async-start | bytes 1048576 | tf_op jit(solution)/shard_map/all_to_all | solution.py:284
  47.3 8.7 %all-to-all-done.ob_ref = bf16[16,128,128]{2,1,0:T(8,128)(2,1)S(1)} async-done(((bf16[16,128,128]{2,1,0:T(8,128)(2,1)}), bf16[16,128,128]{2,1,0:T(8,128)(2,1)S(1)}, u32[]{:S(2)}, u32[]{:S(2)}) %all-to-all-start) | async-done | bytes 524320 | tf_op jit(solution)/shard_map/all_to_all | solution.py:284
  56.0 7.0 %solve.1 = bf16[16,256,128]{2,1,0:T(8,128)(2,1)S(1)} custom-call(bf16[16,128,128]{2,1,0:T(8,128)(2,1)S(1)} %all-to-all-done.ob_ref, bf16[16,256,128]{2,1,0:T(8,128)(2,1)S(1)} %all-to-all-done.1.s_ref, f32[2,128]{1,0:T(2,128)S(1)} %bitcast.11, f32[2,128]{1,0:T(2,128)S(1)} %bitcast.12, s32[1,1]{1,0:T(1,128)S(6)} %copy.11.count_ref), custom_call_target="tpu_custom_call" | custom-call | tf_op jit(solution)/shard_map/solve/pallas_call | solution.py:253
  63.0 19.4 %all_to_all.15.r_ref = bf16[16,256,128]{2,1,0:T(8,128)(2,1)S(1)} all-to-all(bf16[16,256,128]{2,1,0:T(8,128)(2,1)S(1)} %solve.1), channel_id=1, replica_groups=mesh['grp'=16,'tile'=16] {'grp'}, dimensions={0} | all-to-all | bytes 2097152 | tf_op jit(solution)/shard_map/all_to_all | solution.py:284
  82.4 2.8 %turn_out.1 = bf16[4096,128]{1,0:T(8,128)(2,1)} custom-call(bf16[16,256,128]{2,1,0:T(8,128)(2,1)S(1)} %all_to_all.15.r_ref), custom_call_target="tpu_custom_call" | custom-call | tf_op jit(solution)/shard_map/turn_out/pallas_call | solution.py:265
  (16 shorter events, 0.0 us)
Async XLA Ops:
  0.0 6.6 %copy-start.5 = (f32[4]{0:T(128)S(1)}, f32[4]{0:T(128)}, u32[]{:S(2)}) copy-start(f32[4]{0:T(128)} %param.10) | copy-start | bytes 52
  0.0 6.7 %copy-start.6 = (f32[4]{0:T(128)S(1)}, f32[4]{0:T(128)}, u32[]{:S(2)}) copy-start(f32[4]{0:T(128)} %param.11) | copy-start | bytes 52
  0.0 1.6 %copy-start = (f32[64,2,4,8,128]{4,3,2,1,0:T(8,128)S(1)}, f32[64,2,4,8,128]{4,3,2,1,0:T(8,128)}, u32[]{:S(2)}) copy-start(f32[64,2,4,8,128]{4,3,2,1,0:T(8,128)} %param.8) | copy-start | bytes 6291460
  1.6 4.9 %copy-start.4 = (f32[4,128]{1,0:T(4,128)S(1)}, f32[4,128]{1,0:T(4,128)}, u32[]{:S(2)}) copy-start(f32[4,128]{1,0:T(4,128)} %param.9) | copy-start | bytes 6148
  3.1 6.7 %collective-permute-start = (bf16[1024,128]{1,0:T(8,128)(2,1)S(1)}, bf16[1024,128]{1,0:T(8,128)(2,1)S(1)}, u32[]{:S(2)}, u32[]{:S(2)}) collective-permute-start(bf16[1024,128]{1,0:T(8,128)(2,1)S(1)} %get-tuple-element.12), channel_id=1, source_target_pairs={{0,1},{1,2},{2,3},{3,4},{4,5},{5,6},{6,7},{7,8},{8,9},{9,10},{10,1... | collective-permute-start | bytes 786440 | tf_op jit(solution)/shard_map/ppermute | solution.py:302
  6.5 7.0 %collective-permute-start.1 = (bf16[1024,128]{1,0:T(8,128)(2,1)S(1)}, bf16[1024,128]{1,0:T(8,128)(2,1)S(1)}, u32[]{:S(2)}, u32[]{:S(2)}) collective-permute-start(bf16[1024,128]{1,0:T(8,128)(2,1)S(1)} %get-tuple-element.13), channel_id=1, source_target_pairs={{1,0},{2,1},{3,2},{4,3},{5,4},{6,5},{7,6},{8,7},{9,8},{10,9},{11,1... | collective-permute-start | bytes 786440 | tf_op jit(solution)/shard_map/ppermute | solution.py:303
  13.8 11.3 %copy-start.3 = (s32[1,16,256]{2,1,0:T(8,128)S(1)}, s32[1,16,256]{2,1,0:T(8,128)}, u32[]{:S(2)}) copy-start(s32[1,16,256]{2,1,0:T(8,128)} %param.12) | copy-start | bytes 49156
  17.8 22.2 %all-to-all-start.1 = ((bf16[16,256,128]{2,1,0:T(8,128)(2,1)}), bf16[16,256,128]{2,1,0:T(8,128)(2,1)S(1)}, u32[]{:S(2)}, u32[]{:S(2)}) async-start(bf16[16,256,128]{2,1,0:T(8,128)(2,1)} %get-tuple-element.14.s_ref), calls=%async_computation.1 | async-start | bytes 2097152 | tf_op jit(solution)/shard_map/all_to_all | solution.py:284
  24.6 31.4 %copy-start.1 = (f32[1,1,256]{2,1,0:T(1,128)S(1)}, f32[1,1,256]{2,1,0:T(1,128)}, u32[]{:S(2)}) copy-start(f32[1,1,256]{2,1,0:T(1,128)} %param.15) | copy-start | bytes 3076
  24.6 31.4 %copy-start.2 = (f32[1,1,256]{2,1,0:T(1,128)S(1)}, f32[1,1,256]{2,1,0:T(1,128)}, u32[]{:S(2)}) copy-start(f32[1,1,256]{2,1,0:T(1,128)} %param.14) | copy-start | bytes 3076
  24.6 6.7 %collective-permute-start.2 = (bf16[16,128,128]{2,1,0:T(8,128)(2,1)}, bf16[16,128,128]{2,1,0:T(8,128)(2,1)S(1)}, u32[]{:S(2)}, u32[]{:S(2)}) collective-permute-start(bf16[16,128,128]{2,1,0:T(8,128)(2,1)} %get-tuple-element.15), channel_id=1, source_target_pairs={{0,1},{1,2},{2,3},{3,4},{4,5},{5,6},{6,7},{7,8},{8,9},{9,10},{10,1... | collective-permute-start | bytes 1572872 | tf_op jit(solution)/shard_map/ppermute | solution.py:305
  24.9 10.1 %collective-permute-start.3 = (bf16[16,128,128]{2,1,0:T(8,128)(2,1)S(1)}, bf16[16,128,128]{2,1,0:T(8,128)(2,1)S(1)}, u32[]{:S(2)}, u32[]{:S(2)}) collective-permute-start(bf16[16,128,128]{2,1,0:T(8,128)(2,1)S(1)} %get-tuple-element.16), channel_id=1, source_target_pairs={{1,0},{2,1},{3,2},{4,3},{5,4},{6,5},{7,6},{8,7},{9,8},{10,9},{11,1... | collective-permute-start | bytes 1572872 | tf_op jit(solution)/shard_map/ppermute | solution.py:306
  40.0 16.0 %all-to-all-start = ((bf16[16,128,128]{2,1,0:T(8,128)(2,1)}), bf16[16,128,128]{2,1,0:T(8,128)(2,1)S(1)}, u32[]{:S(2)}, u32[]{:S(2)}) async-start(bf16[16,128,128]{2,1,0:T(8,128)(2,1)} %observe.1), calls=%async_computation | async-start | bytes 1048576 | tf_op jit(solution)/shard_map/all_to_all | solution.py:284
where the time goes:
time: 86 us; the launch traced here: 85.2 us
  waiting for transfers between devices  25.2 us (29%)
  Pallas kernels  20.2 us (23%)
  blocking collectives  19.4 us (23%)
  starting transfers between devices  17.4 us (20%)
  local copies, waits for them, and re-layouts  2.18 us (3%)
    all_to_all x1, blocking collectives, exchange(): lax.all_to_all(values, 'grp', split_axis=0, concat_axis=0, tiled=True)  19.4 us
    all_to_all x2, starting transfers between devices, exchange(): lax.all_to_all(values, 'grp', split_axis=0, concat_axis=0, tiled=True)  13.4 us
    all_to_all x2, waiting for transfers between devices, exchange(): lax.all_to_all(values, 'grp', split_axis=0, concat_axis=0, tiled=True)  8.67 us
    pallas_call x1, Pallas kernels, call_solve(): pl.pallas_call(solve, out_shape=jax.ShapeDtypeStruct((16, 256, 128), BF16...  6.99 us
    ppermute x1, waiting for transfers between devices, on_device(): low = lax.ppermute(up, 'tile', forward)  6.11 us
    pallas_call x1, Pallas kernels, call_observe(): pl.pallas_call(observe, out_shape=jax.ShapeDtypeStruct((16, 128, 128), BF...  5.01 us
    pallas_call x1, Pallas kernels, call_forecast(): pl.pallas_call(forecast, out_shape=(jax.ShapeDtypeStruct((16, 256, 128),...  3.99 us
    ppermute x1, waiting for transfers between devices, on_device(): high = lax.ppermute(bottom, 'tile', backward)  3.69 us
  transfers between devices with their start and end apart: 6, of which 5 were waited for; matrix products, arithmetic and copies ran while one was open for 0% of the time, Pallas kernels for 6%

commit v1 on v0

v1 whole, which is shorter than its diff:
```python
import jax
import jax.numpy as jnp
from jax import lax
from jax.experimental import pallas as pl
from jax.experimental.pallas import tpu as pltpu
from jax.sharding import PartitionSpec as P


F32 = jnp.float32
BF16 = jnp.bfloat16
HIGH = lax.Precision.HIGHEST
VMEM = pl.BlockSpec(memory_space=pltpu.VMEM)
SMEM = pl.BlockSpec(memory_space=pltpu.SMEM)
MEMBERS = 1024.0
MESH = pl.DeviceIdType.MESH
ANY = pl.BlockSpec(memory_space=pl.ANY)
PLACE = (2, 0, 1, 3)
PAIR = (1, 2, 0, 3)
SPAN = 130 * 8


def nt(a, b, precision=None):
    return lax.dot_general(a, b, (((1,), (1,)), ((), ())), precision=precision, preferred_element_type=F32)


def nn(a, b, precision=None):
    return lax.dot_general(a, b, (((1,), (0,)), ((), ())), precision=precision, preferred_element_type=F32)


def stencil(ref, k_list, low, high, y0, coef, upper):
    d, u, v = coef
    east_c, west_c, north_c, south_c = d - u, d + u, d - v, d + v
    mid_c = 1.0 - 4.0 * d

    def rows(k, shift):
        return ref[pl.ds(pl.multiple_of(k * SPAN + (y0 + 1 + shift) * 8, 8), 64), :].reshape(8, 8, 128)

    rolled = {}

    def roll(k):
        if k not in rolled:
            rolled[k] = pltpu.roll(rows(k, 0), 4, 1)
        return rolled[k]

    outs = []
    for k in k_list:
        east = jnp.where(upper, roll(k), roll(k + 1)) if k < high else roll(k)
        west = jnp.where(upper, roll(k - 1), roll(k)) if k > low else roll(k)
        outs.append(
            rows(k, 0) * mid_c + east * east_c + west * west_c + rows(k, 1) * north_c + rows(k, -1) * south_c
        )
    return outs


def wrap(ref, k_list):
    for k in k_list:
        ref[k * SPAN:k * SPAN + 8, :] = ref[k * SPAN + 1024:k * SPAN + 1032, :]
        ref[k * SPAN + 1032:k * SPAN + 1040, :] = ref[k * SPAN + 8:k * SPAN + 16, :]


def turn_in(x_ref, field, rows):
    for row in rows:
        for level in range(4):
            plane = jnp.concatenate(
                [x_ref[level, pl.ds(row, 64, stride=16), :], x_ref[level, pl.ds(8 + row, 64, stride=16), :]], axis=0
            )
            start = (row // 2 + 1) * SPAN + 8 + (row % 2) * 4 + level
            field[pl.ds(start, 128, stride=8), :] = plane.T


def forward(
    x_hbm, d_ref, u_ref, v_ref, cell_ref, ob_ref, dev_ref, centre_ref,
    x_ref, first, second, halo_out, halo_in, mine, blocked, region, seen, seen_out,
    load_sem, halo_send, halo_recv, state_send, state_recv, region_send, region_recv, ob_send, ob_recv,
):
    me = lax.axis_index("grp")
    tile = lax.axis_index("tile")
    tiles = lax.axis_size("tile")
    below, above = lax.rem(tile + tiles - 1, tiles), lax.rem(tile + 1, tiles)

    def other(i):
        return lax.rem(me + 1 + i, 16)

    loads = []
    for level in range(4):
        loads.append(pltpu.make_async_copy(x_hbm.at[:, level], x_ref.at[level].reshape(128, 8, 128), load_sem.at[level]))
        loads[-1].start()
    barrier = pltpu.get_barrier_semaphore()

    @pl.loop(0, 15)
    def _(i):
        pl.semaphore_signal(barrier, inc=1, device_id=(other(i), tile), device_id_type=MESH)

    pl.semaphore_signal(barrier, inc=1, device_id=(me, below), device_id_type=MESH)
    pl.semaphore_signal(barrier, inc=1, device_id=(me, above), device_id_type=MESH)

    def halo(side):
        return pltpu.make_async_remote_copy(
            src_ref=halo_out.at[side], dst_ref=halo_in.at[side], send_sem=halo_send.at[side],
            recv_sem=halo_recv.at[side], device_id=(me, above if side == 0 else below), device_id_type=MESH,
        )

    def state(i, part):
        rows = pl.ds(part * 128, 128)
        return pltpu.make_async_remote_copy(
            src_ref=mine.at[other(i), rows], dst_ref=blocked.at[me, rows], send_sem=state_send.at[part, i],
            recv_sem=state_recv.at[part, i], device_id=(other(i), tile), device_id_type=MESH,
        )

    def edge(k):
        return pltpu.make_async_remote_copy(
            src_ref=mine.at[:, pl.ds(PLACE[k] * 64, 64)], dst_ref=region.at[k], send_sem=region_send.at[k],
            recv_sem=region_recv.at[k], device_id=(me, above if k > 1 else below), device_id_type=MESH,
        )

    def seen_copy(i):
        return pltpu.make_async_remote_copy(
            src_ref=seen_out.at[other(i)], dst_ref=ob_ref.at[me], send_sem=ob_send.at[i],
            recv_sem=ob_recv.at[i], device_id=(other(i), tile), device_id_type=MESH,
        )

    for load in loads:
        load.wait()
    turn_in(x_ref, first, (0, 1, 6, 7))
    halo_out[1] = first[SPAN + 8:SPAN + 1032, :].astype(BF16)
    halo_out[0] = first[4 * SPAN + 8:4 * SPAN + 1032, :].astype(BF16)
    pl.semaphore_wait(barrier, 17)
    halo(0).start()
    halo(1).start()
    turn_in(x_ref, first, (2, 3, 4, 5))
    wrap(first, (1, 2, 3, 4))
    upper = lax.broadcasted_iota(jnp.int32, (8, 8, 128), 1) < 4
    u = 0.5 * u_ref[...][None]
    v = 0.5 * v_ref[...][None]

    def coef(y0):
        return d_ref[pl.ds(y0, 8)], u, v

    def advance(k_list, low, high):
        @pl.loop(0, 16)
        def _(step):
            y0 = step * 8
            for k, value in zip(k_list, stencil(first, k_list, low, high, y0, coef(y0), upper)):
                second[pl.ds(pl.multiple_of(k * SPAN + (y0 + 1) * 8, 8), 64), :] = value.reshape(64, 128)

    def finish(k_list, part):
        def one(b):
            y0 = b * 8
            for k, value in zip(k_list, stencil(second, k_list, 0, 5, y0, coef(y0), upper)):
                place = PLACE[k - 1] * 64
                mine[b, place:place + 64, :] = value.reshape(64, 128).astype(BF16)

        one(other(0))

        @pl.loop(1, 15)
        def _(i):
            one(other(i))
            state(i - 1, part).start()

        one(me)
        state(14, part).start()
        blocked[me, part * 128:part * 128 + 128, :] = mine[me, part * 128:part * 128 + 128, :]

    advance((1, 2, 3, 4), 1, 4)
    wrap(second, (2, 3))
    finish((2, 3), 0)
    edge(1).start()
    edge(2).start()
    for side in (0, 1):
        halo(side).wait()
        k = 5 * side
        first[k * SPAN + 8:k * SPAN + 1032, :] = halo_in[side].astype(F32)
    wrap(first, (0, 5))
    advance((0, 1, 4, 5), 0, 5)
    wrap(second, (1, 4))
    finish((1, 4), 1)
    edge(0).start()
    edge(3).start()

    cell = cell_ref[...]
    level_index = cell // 256
    rest = cell % 256
    row = rest // 16
    col = rest % 16
    half = level_index // 4
    index = (row // 2) * 128 + col * 8 + (row % 2) * 4 + level_index % 4
    lane = lax.broadcasted_iota(jnp.int32, (256, 128), 1)
    left = lane < 64

    def pick(i, kk_list):
        b = other(i)
        before, after = lax.rem(b + 15, 16), lax.rem(b + 1, 16)
        picks, pieces = [], []
        for kk in kk_list:
            picks.append(jnp.where(index[:, i:i + 1] == lane + kk * 128, 1.0, 0.0).astype(BF16))
            if 2 <= kk < 6:
                place = PLACE[kk - 2] * 64
                pieces.append(mine[before, place + 32:place + 64, :])
                pieces.append(mine[b, place:place + 64, :])
                pieces.append(mine[after, place:place + 32, :])
            else:
                k = kk + 2 if kk < 2 else kk - 6
                pieces.append(region[k, before, 32:64, :])
                pieces.append(region[k, b, :, :])
                pieces.append(region[k, after, 0:32, :])
        return nn(jnp.concatenate(picks, axis=1), jnp.concatenate(pieces, axis=0))

    for i in range(16):
        seen[i] = pick(i, (2, 3, 4, 5))
    for k in (1, 2, 0, 3):
        edge(k).wait()
    for i in range(16):
        values = seen[i] + pick(i, (0, 1, 6, 7))
        values = jnp.where((half[:, i:i + 1] == 0) == left, values, 0.0)
        values = values + pltpu.roll(values, 64, 1)
        packed = jnp.where(left[0:128], values[0:128], values[128:256]).astype(BF16)
        if i < 15:
            seen_out[other(i)] = packed
        else:
            ob_ref[me] = packed
        if i > 0:
            seen_copy(i - 1).start()

    for part in range(2):
        @pl.loop(0, 15)
        def _(i):
            state(i, part).wait()

    total = blocked[0].astype(F32)
    for g in range(1, 16):
        total = total + blocked[g].astype(F32)
    centre0 = jnp.sum(jnp.where(left, total, 0.0), axis=1, keepdims=True) * (1.0 / MEMBERS)
    centre1 = jnp.sum(jnp.where(left, 0.0, total), axis=1, keepdims=True) * (1.0 / MEMBERS)
    centre = jnp.where(left, centre0, centre1)
    centre_ref[...] = centre
    for i in range(16):
        dev_ref[:, i * 128:(i + 1) * 128] = (blocked[other(i)].astype(F32) - centre).astype(BF16)

    @pl.loop(0, 15)
    def _(i):
        seen_copy(i).wait()


def backward(
    ob_ref, dev_ref, centre_ref, weight_ref, value_ref, count_ref, out_ref, basis, sending, send_sem, recv_sem
):
    me = lax.axis_index("grp")
    tile = lax.axis_index("tile")

    def other(i):
        return lax.rem(me + 1 + i, 16)

    barrier = pltpu.get_barrier_semaphore()

    @pl.loop(0, 15)
    def _(i):
        pl.semaphore_signal(barrier, inc=1, device_id=(other(i), tile), device_id_type=MESH)

    def result(i, part):
        rows = pl.ds(part * 128, 128)
        return pltpu.make_async_remote_copy(
            src_ref=sending.at[other(i), rows], dst_ref=out_ref.at[me, rows], send_sem=send_sem.at[part, i],
            recv_sem=recv_sem.at[part, i], device_id=(other(i), tile), device_id_type=MESH,
        )

    left = lax.broadcasted_iota(jnp.int32, (128, 128), 1) < 64
    left2 = lax.broadcasted_iota(jnp.int32, (256, 128), 1) < 64
    total = ob_ref[0].astype(F32)
    for g in range(1, 16):
        total = total + ob_ref[g].astype(F32)
    mean0 = jnp.sum(jnp.where(left, total, 0.0), axis=1, keepdims=True) * (1.0 / MEMBERS)
    mean1 = jnp.sum(jnp.where(left, 0.0, total), axis=1, keepdims=True) * (1.0 / MEMBERS)
    count = count_ref[0, 0]
    row_lane = lax.broadcasted_iota(jnp.int32, (1, 128), 1)
    root0 = jnp.sqrt(jnp.where(row_lane < count, weight_ref[0:1, :], 0.0))
    root1 = jnp.sqrt(jnp.where(row_lane + 128 < count, weight_ref[1:2, :], 0.0))
    root0 = jnp.broadcast_to(root0, (128, 128)).T
    root1 = jnp.broadcast_to(root1, (128, 128)).T
    target0 = jnp.broadcast_to(value_ref[0:1, :], (128, 128)).T
    target1 = jnp.broadcast_to(value_ref[1:2, :], (128, 128)).T
    misfit = jnp.concatenate([root0 * (target0 - mean0), root1 * (target1 - mean1)], axis=0)
    mean = jnp.where(left, mean0, mean1)
    root = jnp.where(left, root0, root1)
    for i in range(16):
        scaled = (ob_ref[other(i)].astype(F32) - mean) * root
        turned = pltpu.roll(scaled, 64, 1)
        both = jnp.concatenate(
            [jnp.where(left, scaled, turned), jnp.where(left, turned, scaled)], axis=0
        )
        basis[0:256, i * 128:(i + 1) * 128] = jnp.where(left2, both, 0.0).astype(BF16)
        basis[256:512, i * 128:(i + 1) * 128] = jnp.where(left2, 0.0, both).astype(BF16)
    small = nt(basis[0:256, :], basis[0:256, :])
    eye = lax.broadcasted_iota(jnp.int32, (256, 256), 0) == lax.broadcasted_iota(jnp.int32, (256, 256), 1)
    trace = jnp.sum(jnp.where(eye, small, 0.0), axis=(0, 1), keepdims=True)
    s = (MEMBERS - 1.0) + trace * (1.0 / MEMBERS)
    inv_s = 1.0 / s
    inv_root_s = lax.rsqrt(s)
    a = (MEMBERS - 1.0) * inv_s
    p = 1.5 - 0.5 * a
    r0 = 1.5 * p - 0.5 * a * p * p * p
    r1 = -0.75 - 0.5 * p * p * p + 0.75 * a * p * p
    r2 = 0.5 * (1.5 * p * p - 0.75 * a * p)
    r3 = (1.0 / 6.0) * (0.375 * a - 2.25 * p)
    r4 = 1.5 / 24.0
    g1 = small * inv_s
    g2 = nn(g1, g1, HIGH)
    q = jnp.where(eye, r1, 0.0) + r2 * g1 + r3 * g2 + r4 * nn(g2, g1, HIGH)
    first = (r0 * misfit + nn(g1, nn(q, misfit, HIGH), HIGH)) * inv_root_s
    gain = (r0 * first + nn(g1, nn(q, first, HIGH), HIGH)) * inv_root_s
    spread = jnp.sqrt(jnp.full((1, 1), MEMBERS - 1.0, F32))
    mix = q * (spread * inv_s * inv_root_s)
    keep = r0 * spread * inv_root_s
    cross = nt(dev_ref[...], basis[...])
    cross0, cross1 = cross[:, 0:256], cross[:, 256:512]
    update = jnp.concatenate([nn(cross0, mix, HIGH), nn(cross1, mix, HIGH)], axis=1).astype(BF16)
    offset = centre_ref[...] + jnp.where(left2, nn(cross0, gain, HIGH), nn(cross1, gain, HIGH))
    pl.semaphore_wait(barrier, 15)
    for part in range(2):
        rows = slice(part * 128, part * 128 + 128)
        for i in range(16):
            lanes = slice(i * 128, (i + 1) * 128)
            value = offset[rows] + keep * dev_ref[rows, lanes].astype(F32) + nn(update[rows], basis[:, lanes])
            if i < 15:
                sending[other(i), rows, :] = value.astype(BF16)
            else:
                out_ref[me, rows, :] = value.astype(BF16)
            if i > 0:
                result(i - 1, part).start()
    for part in range(2):
        @pl.loop(0, 15)
        def _(i):
            result(i, part).wait()


def turn_out(r_ref, out_ref, field, stage):
    for b in range(16):
        for place in range(4):
            field[pl.ds(PAIR[place] * 1024 + b * 64, 64), :] = r_ref[b, place * 64:(place + 1) * 64, :].astype(F32)
    for row in range(8):
        for level in range(4):
            start = level * 8 + row
            plane = field[pl.ds((row // 2) * 1024 + (row % 2) * 4 + level, 128, stride=8), :].T
            stage[pl.ds(start, 64, stride=64), :] = plane[0:64]
            stage[pl.ds(start + 32, 64, stride=64), :] = plane[64:128]
    out_ref[...] = stage[...].astype(BF16)


def params(collective=None, mib=30):
    if collective is None:
        return pltpu.CompilerParams(vmem_limit_bytes=mib * 1024 * 1024)
    return pltpu.CompilerParams(
        vmem_limit_bytes=mib * 1024 * 1024, collective_id=collective, has_side_effects=True
    )


def call_forward(x, d, u, v, cell):
    dma = pltpu.SemaphoreType.DMA
    return pl.pallas_call(
        forward,
        out_shape=(
            jax.ShapeDtypeStruct((16, 128, 128), BF16),
            jax.ShapeDtypeStruct((256, 2048), BF16),
            jax.ShapeDtypeStruct((256, 128), F32),
        ),
        in_specs=[ANY, VMEM, VMEM, VMEM, VMEM],
        out_specs=(VMEM, VMEM, VMEM),
        scratch_shapes=[
            pltpu.VMEM((4, 1024, 128), F32),
            pltpu.VMEM((6 * SPAN, 128), F32),
            pltpu.VMEM((6 * SPAN, 128), F32),
            pltpu.VMEM((2, 1024, 128), BF16),
            pltpu.VMEM((2, 1024, 128), BF16),
            pltpu.VMEM((16, 256, 128), BF16),
            pltpu.VMEM((16, 256, 128), BF16),
            pltpu.VMEM((4, 16, 64, 128), BF16),
            pltpu.VMEM((16, 256, 128), F32),
            pltpu.VMEM((16, 128, 128), BF16),
            dma((4,)), dma((2,)), dma((2,)), dma((2, 15)), dma((2, 15)), dma((4,)), dma((4,)), dma((15,)), dma((15,)),
        ],
        compiler_params=params(0),
        name="forward",
    )(x, d, u, v, cell)


def call_backward(ob, dev, centre, weight, value, count):
    dma = pltpu.SemaphoreType.DMA
    return pl.pallas_call(
        backward,
        out_shape=jax.ShapeDtypeStruct((16, 256, 128), BF16),
        in_specs=[VMEM, VMEM, VMEM, VMEM, VMEM, SMEM],
        out_specs=VMEM,
        scratch_shapes=[
            pltpu.VMEM((512, 2048), BF16),
            pltpu.VMEM((16, 256, 128), BF16),
            dma((2, 15)), dma((2, 15)),
        ],
        compiler_params=params(1),
        name="backward",
    )(ob, dev, centre, weight, value, count)


def call_turn_out(r):
    return pl.pallas_call(
        turn_out,
        out_shape=jax.ShapeDtypeStruct((4096, 128), BF16),
        in_specs=[VMEM],
        out_specs=VMEM,
        scratch_shapes=[pltpu.VMEM((4096, 128), F32), pltpu.VMEM((4096, 128), F32)],
        compiler_params=params(),
        name="turn_out",
    )(r)


def coefficients(diffusivity, eastward_velocity, northward_velocity):
    d = jnp.broadcast_to(jnp.concatenate([diffusivity, diffusivity], 0).T[:, :, None], (128, 8, 128))
    u = jnp.broadcast_to(jnp.concatenate([eastward_velocity] * 2)[:, None], (8, 128))
    v = jnp.broadcast_to(jnp.concatenate([northward_velocity] * 2)[:, None], (8, 128))
    return d, u, v


def on_device(
    starting_realizations,
    diffusivity,
    eastward_velocity,
    northward_velocity,
    obs_cell,
    obs_count,
    obs_value,
    obs_weight,
):
    d, u, v = coefficients(diffusivity, eastward_velocity, northward_velocity)
    cell = obs_cell[0]
    cell = lax.dynamic_slice_in_dim(jnp.concatenate([cell, cell]), lax.axis_index("grp") + 1, 16, 0).T
    measured, deviation, centre = call_forward(starting_realizations.reshape(128, 4, 8, 128), d, u, v, cell)
    updated = call_backward(
        measured, deviation, centre, obs_weight.reshape(2, 128), obs_value.reshape(2, 128), obs_count
    )
    return call_turn_out(updated).reshape(64, 2, 4, 8, 128)


def solution(mesh):
    return jax.shard_map(
        on_device,
        mesh=mesh,
        in_specs=(
            P("grp", None, None, "tile", None),
            P(),
            P(),
            P(),
            P("tile", None, None),
            P("tile", "grp"),
            P("tile", "grp", None),
            P("tile", "grp", None),
        ),
        out_specs=P("grp", None, None, "tile", None),
        check_vma=False,
    )
```

time: 86 us -> 62.6 us (0.73)
  Pallas kernels: 20.2 us -> 56.3 us
  waiting for transfers between devices: 25.2 us -> 0 us
  blocking collectives: 19.4 us -> 0 us
  starting transfers between devices: 17.4 us -> 0 us
  other arithmetic: 0.16 us -> 3.16 us
    pallas_call x4 -> x2, Pallas kernels: 17.4 us -> 53.5 us  [the longest x1 29.6 us: call_forward(): pl.pallas_call(forward, out_shape=(jax.ShapeDtypeStruct((16, 128, 128), B...]
    all_to_all x1 -> x0, blocking collectives: 19.4 us -> none  [exchange(): lax.all_to_all(values, 'grp', split_axis=0, concat_axis=0, tiled=True)]
    ppermute x4 -> x0, waiting for transfers between devices: 16.5 us -> none  [the longest x1 6.11 us: on_device(): low = lax.ppermute(up, 'tile', forward)]
    all_to_all x2 -> x0, starting transfers between devices: 13.4 us -> none  [exchange(): lax.all_to_all(values, 'grp', split_axis=0, concat_axis=0, tiled=True)]
    all_to_all x2 -> x0, waiting for transfers between devices: 8.67 us -> none  [exchange(): lax.all_to_all(values, 'grp', split_axis=0, concat_axis=0, tiled=True)]
    ppermute x4 -> x0, starting transfers between devices: 3.95 us -> none  [the longest x1 3.42 us: on_device(): low = lax.ppermute(top, 'tile', forward)]
    unnamed x15 -> x7, local copies, waits for them, and re-layouts: 1.74 us -> 1.7 us
  transfers between devices with their start and end apart: 6 -> 0, of which waited for: 5 -> 0; matrix products, arithmetic and copies ran while one was open for 0% -> 0% of each run, Pallas kernels for 6% -> 0%
where the time goes in v1:
time: 62.6 us; the launch traced here: 62.3 us
  Pallas kernels  56.3 us (90%)
  other arithmetic  3.16 us (5%)
  local copies, waits for them, and re-layouts  2.13 us (3%)
  between operations  0.73 us (1%)
    pallas_call x1, Pallas kernels, call_forward(): pl.pallas_call(forward, out_shape=(jax.ShapeDtypeStruct((16, 128, 128), B...  29.6 us
    pallas_call x1, Pallas kernels, call_backward(): pl.pallas_call(backward, out_shape=jax.ShapeDtypeStruct((16, 256, 128), B...  23.9 us
    pallas_call x1, Pallas kernels, call_turn_out(): pl.pallas_call(turn_out, out_shape=jax.ShapeDtypeStruct((4096, 128), BF16...  2.8 us
    unnamed x7, local copies, waits for them, and re-layouts  1.7 us

profile of v1, /device:TPU:97, one launch (start us, length us, event | category | flops | bytes accessed | tf_op | source)
XLA Modules:
  0.0 62.3 jit_solution(16709023586458016183)
XLA Ops:
  0.0 0.0 copy-start.1
  0.0 0.0 copy-start.2
  0.7 0.8 %pad_maximum_fusion = f32[8]{0:T(128)S(1)} fusion(f32[4]{0:T(128)} %param.10), kind=kLoop, calls=%fused_computation.4 | loop fusion | flops 8 | bytes 48 | tf_op jit(solution)/shard_map/concatenate | solution.py:416
  1.5 0.8 %pad_maximum_fusion.1 = f32[8]{0:T(128)S(1)} fusion(f32[4]{0:T(128)} %param.11), kind=kLoop, calls=%fused_computation.5 | loop fusion | flops 8 | bytes 48 | tf_op jit(solution)/shard_map/concatenate | solution.py:417
  2.3 0.1 broadcast_in_dim.8.v_ref
  2.4 0.1 broadcast_in_dim.7.u_ref
  2.4 0.8 %maximum_bitcast_fusion = f32[128,8]{0,1:T(8,128)S(1)} fusion(f32[4,128]{1,0:T(4,128)} %param.9), kind=kLoop, calls=%fused_computation.3 | loop fusion | flops 1024 | bytes 6144 | tf_op jit(solution)/shard_map/transpose | solution.py:415
  3.2 0.8 %fusion = s32[16,256]{1,0:T(8,128)S(1)} fusion(s32[]{:T(128)S(6)} %select_n.3, s32[16,256]{1,0:T(8,128)} %bitcast.12), kind=kLoop, calls=%fused_computation.2 | loop fusion | flops 4096 | bytes 32772 | tf_op jit(solution)/shard_map/concatenate | solution.py:433
  4.0 0.1 copy.11
  4.1 0.1 copy.13
  4.2 0.2 broadcast_in_dim.6.d_ref
  4.4 0.0 copy-start
  4.4 1.6 %copy-done = f32[64,2,4,8,128]{4,3,2,1,0:T(8,128)S(1)} copy-done((f32[64,2,4,8,128]{4,3,2,1,0:T(8,128)S(1)}, f32[64,2,4,8,128]{4,3,2,1,0:T(8,128)}, u32[]{:S(2)}) %copy-start) | copy-done | bytes 2097176
  6.0 29.6 %forward.1 = (bf16[16,128,128]{2,1,0:T(8,128)(2,1)S(1)}, bf16[256,2048]{1,0:T(8,128)(2,1)S(1)}, f32[256,128]{1,0:T(8,128)S(1)}) custom-call(f32[128,4,8,128]{3,2,1,0:T(8,128)S(1)} %bitcast.8, f32[128,8,128]{2,1,0:T(8,128)S(1)} %broadcast_in_dim.6.d_ref, f32[8,128]{1,0:T(8,128)S(1)} %broadcast_in_dim.7.u_ref, f32[8,128]{1,0:T(8,128)S(1)} %broadcast_in_dim.8.v_ref, ...), custom_call_target="tpu_custom_call" | custom-call | tf_op jit(solution)/shard_map/forward/pallas_call | solution.py:358
  35.6 0.0 copy-done.1
  35.6 0.0 copy-done.2
  35.6 23.9 %backward.1.r_ref = bf16[16,256,128]{2,1,0:T(8,128)(2,1)S(1)} custom-call(bf16[16,128,128]{2,1,0:T(8,128)(2,1)S(1)} %get-tuple-element.8.ob_ref, bf16[256,2048]{1,0:T(8,128)(2,1)S(1)} %get-tuple-element.9.dev_ref, f32[256,128]{1,0:T(8,128)S(1)} %get-tuple-element.10.centre_ref, f32[2,128]{1,0:T(2,128)S(1)} %bitcast.10, f32[2,128]{1,0:T(2,128)S(1)} %bitcast.11, ...), custom_call_target="tpu_custom_call" | custom-call | tf_op jit(solution)/shard_map/backward/pallas_call | solution.py:387
  59.5 2.8 %turn_out.1 = bf16[4096,128]{1,0:T(8,128)(2,1)} custom-call(bf16[16,256,128]{2,1,0:T(8,128)(2,1)S(1)} %backward.1.r_ref), custom_call_target="tpu_custom_call" | custom-call | tf_op jit(solution)/shard_map/turn_out/pallas_call | solution.py:403
Async XLA Ops:
  0.0 35.6 %copy-start.1 = (f32[1,1,256]{2,1,0:T(1,128)S(1)}, f32[1,1,256]{2,1,0:T(1,128)}, u32[]{:S(2)}) copy-start(f32[1,1,256]{2,1,0:T(1,128)} %param.15) | copy-start | bytes 3076
  0.0 35.6 %copy-start.2 = (f32[1,1,256]{2,1,0:T(1,128)S(1)}, f32[1,1,256]{2,1,0:T(1,128)}, u32[]{:S(2)}) copy-start(f32[1,1,256]{2,1,0:T(1,128)} %param.14) | copy-start | bytes 3076
  4.4 1.6 %copy-start = (f32[64,2,4,8,128]{4,3,2,1,0:T(8,128)S(1)}, f32[64,2,4,8,128]{4,3,2,1,0:T(8,128)}, u32[]{:S(2)}) copy-start(f32[64,2,4,8,128]{4,3,2,1,0:T(8,128)} %param.8) | copy-start | bytes 6291460

commit v2 on v1

v2 whole, which is shorter than its diff:
```python
import jax
import jax.numpy as jnp
from jax import lax
from jax.experimental import pallas as pl
from jax.experimental.pallas import tpu as pltpu
from jax.sharding import PartitionSpec as P


F32 = jnp.float32
BF16 = jnp.bfloat16
VMEM = pl.BlockSpec(memory_space=pltpu.VMEM)
MEMBERS = 1024.0
MESH = pl.DeviceIdType.MESH
ANY = pl.BlockSpec(memory_space=pl.ANY)
PLACE = (2, 0, 1, 3)
PAIR = (1, 2, 0, 3)
SPAN = 130 * 8


def nt(a, b):
    return lax.dot_general(a, b, (((1,), (1,)), ((), ())), preferred_element_type=F32)


def nn(a, b):
    return lax.dot_general(a, b, (((1,), (0,)), ((), ())), preferred_element_type=F32)


def split(a):
    top = a.astype(BF16)
    return top, (a - top.astype(F32)).astype(BF16)


def nn3(a, b):
    (a0, a1), (b0, b1) = a, b
    return nn(jnp.concatenate([a0, a0, a1], axis=1), jnp.concatenate([b0, b1, b0], axis=0))


def stencil(ref, k_list, low, high, y0, coef, upper):
    d, u, v = coef
    east_c, west_c, north_c, south_c = d - u, d + u, d - v, d + v
    mid_c = 1.0 - 4.0 * d

    def rows(k, shift):
        return ref[pl.ds(pl.multiple_of(k * SPAN + (y0 + 1 + shift) * 8, 8), 64), :].reshape(8, 8, 128)

    rolled = {}

    def roll(k):
        if k not in rolled:
            rolled[k] = pltpu.roll(rows(k, 0), 4, 1)
        return rolled[k]

    outs = []
    for k in k_list:
        east = jnp.where(upper, roll(k), roll(k + 1)) if k < high else roll(k)
        west = jnp.where(upper, roll(k - 1), roll(k)) if k > low else roll(k)
        outs.append(
            rows(k, 0) * mid_c + east * east_c + west * west_c + rows(k, 1) * north_c + rows(k, -1) * south_c
        )
    return outs


def wrap(ref, k_list):
    for k in k_list:
        ref[k * SPAN:k * SPAN + 8, :] = ref[k * SPAN + 1024:k * SPAN + 1032, :]
        ref[k * SPAN + 1032:k * SPAN + 1040, :] = ref[k * SPAN + 8:k * SPAN + 16, :]


def turn_in(x_ref, field, rows):
    for row in rows:
        for level in range(4):
            start = level * 8 + row
            plane = jnp.concatenate(
                [x_ref[pl.ds(start, 64, stride=64), :], x_ref[pl.ds(start + 32, 64, stride=64), :]], axis=0
            )
            start = (row // 2 + 1) * SPAN + 8 + (row % 2) * 4 + level
            field[pl.ds(start, 128, stride=8), :] = plane.T


def turn_out(returned, field, stage, place):
    k = PAIR[place]
    for b in range(16):
        field[k * 1024 + b * 64:k * 1024 + b * 64 + 64, :] = returned[b, place * 64:place * 64 + 64, :].astype(F32)
    for row in (2 * k, 2 * k + 1):
        for level in range(4):
            start = level * 8 + row
            plane = field[pl.ds(k * 1024 + (row % 2) * 4 + level, 128, stride=8), :].T
            stage[pl.ds(start, 64, stride=64), :] = plane[0:64]
            stage[pl.ds(start + 32, 64, stride=64), :] = plane[64:128]


def whole(
    x_hbm, d_hbm, u_hbm, v_hbm, cell_hbm, weight_hbm, value_hbm, count_ref, out_ref,
    d_ref, u_ref, v_ref, cell_ref, weight_ref, value_ref, small_sem, x_ref, first, second, spread_d, cells, hot, halo_out, halo_in, mine, blocked, region, seen, seen_out, measured,
    dev, basis, sending, returned,
    load_sem, halo_send, halo_recv, state_send, state_recv, late_send, late_recv, region_send, region_recv,
    ob_send, ob_recv, back_send, back_recv,
):
    me = lax.axis_index("grp")
    tile = lax.axis_index("tile")
    tiles = lax.axis_size("tile")
    below, above = lax.rem(tile + tiles - 1, tiles), lax.rem(tile + 1, tiles)

    def other(i):
        return lax.rem(me + 1 + i, 16)

    small_loads = []
    for source, target in (
        (d_hbm, d_ref), (u_hbm, u_ref), (v_hbm, v_ref), (cell_hbm, cell_ref), (weight_hbm, weight_ref),
        (value_hbm, value_ref),
    ):
        small_loads.append(pltpu.make_async_copy(source, target, small_sem.at[len(small_loads)]))
        small_loads[-1].start()
    loads = []
    for piece in range(4):
        rows = pl.ds(piece * 1024, 1024)
        loads.append(pltpu.make_async_copy(x_hbm.at[rows], x_ref.at[rows], load_sem.at[piece]))
        loads[-1].start()
    barrier = pltpu.get_barrier_semaphore()

    @pl.loop(0, 15)
    def _(i):
        pl.semaphore_signal(barrier, inc=1, device_id=(other(i), tile), device_id_type=MESH)

    pl.semaphore_signal(barrier, inc=1, device_id=(me, below), device_id_type=MESH)
    pl.semaphore_signal(barrier, inc=1, device_id=(me, above), device_id_type=MESH)

    def remote(source, target, send, recv, device):
        return pltpu.make_async_remote_copy(
            src_ref=source, dst_ref=target, send_sem=send, recv_sem=recv, device_id=device, device_id_type=MESH
        )

    def halo(side):
        return remote(
            halo_out.at[side], halo_in.at[side], halo_send.at[side], halo_recv.at[side],
            (me, above if side == 0 else below),
        )

    def state(i):
        rows = pl.ds(0, 128)
        return remote(
            mine.at[other(i), rows], blocked.at[me, rows], state_send.at[i], state_recv.at[i], (other(i), tile)
        )

    def late(i, part):
        rows = pl.ds(128 + 64 * part, 64)
        return remote(
            mine.at[other(i), rows], blocked.at[me, rows], late_send.at[part, i], late_recv.at[part, i],
            (other(i), tile),
        )

    def edge(k):
        return remote(
            mine.at[:, pl.ds(PLACE[k] * 64, 64)], region.at[k], region_send.at[k], region_recv.at[k],
            (me, above if k > 1 else below),
        )

    def seen_copy(i):
        return remote(seen_out.at[other(i)], measured.at[me], ob_send.at[i], ob_recv.at[i], (other(i), tile))

    def back(i, place):
        rows = pl.ds(place * 64, 64)
        return remote(
            sending.at[other(i), rows], returned.at[me, rows], back_send.at[place, i], back_recv.at[place, i],
            (other(i), tile),
        )

    for load in loads:
        load.wait()
    turn_in(x_ref, first, (0, 1, 6, 7))
    halo_out[1] = first[SPAN + 8:SPAN + 1032, :].astype(BF16)
    halo_out[0] = first[4 * SPAN + 8:4 * SPAN + 1032, :].astype(BF16)
    pl.semaphore_wait(barrier, 17)
    halo(0).start()
    halo(1).start()

    for load in small_loads:
        load.wait()
    sub = lax.broadcasted_iota(jnp.int32, (8, 128), 0)
    u = jnp.zeros((8, 128), F32)
    v = jnp.zeros((8, 128), F32)
    for level in range(4):
        column = jnp.broadcast_to(d_ref[level:level + 1, :], (128, 128)).T
        spread_d[pl.ds(level, 128, stride=8), :] = column
        spread_d[pl.ds(level + 4, 128, stride=8), :] = column
        here = lax.rem(sub, 4) == level
        u = jnp.where(here, 0.5 * u_ref[level], u)
        v = jnp.where(here, 0.5 * v_ref[level], v)
    turn_in(x_ref, first, (2, 3, 4, 5))
    wrap(first, (1, 2, 3, 4))
    upper = lax.broadcasted_iota(jnp.int32, (8, 8, 128), 1) < 4

    def coef(y0):
        return spread_d[pl.ds(pl.multiple_of(y0 * 8, 64), 64), :].reshape(8, 8, 128), u[None], v[None]

    def finish(k_list, send, before=None):
        def one(b):
            y0 = b * 8
            for k, value in zip(k_list, stencil(second, k_list, 0, 5, y0, coef(y0), upper)):
                place = PLACE[k - 1] * 64
                mine[b, place:place + 64, :] = value.reshape(64, 128).astype(BF16)

        one(other(0))

        @pl.loop(1, 14)
        def _(i):
            if before is not None:
                before(i + 2)
            one(other(i))
            send(i - 1).start()

        one(other(14))
        send(13).start()
        one(me)
        send(14).start()

    def inner(ahead):
        block = lax.rem(me + ahead, 16)
        y0 = block * 8
        for k, value in zip((1, 2, 3, 4), stencil(first, (1, 2, 3, 4), 1, 4, y0, coef(y0), upper)):
            second[pl.ds(pl.multiple_of(k * SPAN + (y0 + 1) * 8, 8), 64), :] = value.reshape(64, 128)

        @pl.when(block == 0)
        def _():
            for k in (2, 3):
                second[k * SPAN + 1032:k * SPAN + 1040, :] = second[k * SPAN + 8:k * SPAN + 16, :]

        @pl.when(block == 15)
        def _():
            for k in (2, 3):
                second[k * SPAN:k * SPAN + 8, :] = second[k * SPAN + 1024:k * SPAN + 1032, :]

    @pl.loop(0, 3)
    def _(ahead):
        inner(ahead)

    finish((2, 3), state, inner)
    edge(1).start()
    edge(2).start()

    for i in range(16):
        cell = cell_ref[pl.ds(other(i), 1), :]
        place = cell % 256
        row, col = place // 16, place % 16
        level = cell // 256
        pair = row // 2
        own = (pair >= 2) & (pair <= 5)
        group = jnp.where(own, (pair - 2) // 2, jnp.where((pair == 0) | (pair == 7), 2, 3))
        second_of = jnp.where(own, pair % 2, jnp.where(pair >= 6, 1, 0))
        cells[0, i:i + 1, :] = (second_of * 128 + col * 8 + (row % 2) * 4 + level % 4).astype(F32)
        cells[1, i:i + 1, :] = (group + 4 * (level // 4)).astype(F32)
    index = jnp.concatenate([cells[0, :, 0:128].T, cells[0, :, 128:256].T], axis=0)
    choice = jnp.concatenate([cells[1, :, 0:128].T, cells[1, :, 128:256].T], axis=0)
    count = count_ref[0, 0]
    row_lane = lax.broadcasted_iota(jnp.int32, (1, 128), 1)
    root_rows, roots = [], []
    for part in range(2):
        root = jnp.sqrt(jnp.where(row_lane + 128 * part < count, weight_ref[part:part + 1, :], 0.0))
        root_rows.append(root)
        roots.append(jnp.broadcast_to(root, (128, 128)).T)

    for side in (0, 1):
        halo(side).wait()
        k = 5 * side
        first[k * SPAN + 8:k * SPAN + 1032, :] = halo_in[side].astype(F32)
    wrap(first, (0, 5))

    @pl.loop(0, 16)
    def _(step):
        y0 = step * 8
        d, u_c, v_c = coef(y0)
        for upper_k, lower_k, east_k, west_k, own in ((1, 0, 1, 0, 1), (5, 4, 5, 4, 4)):
            def rows(k, shift):
                return first[pl.ds(pl.multiple_of(k * SPAN + (y0 + 1 + shift) * 8, 8), 64), :].reshape(8, 8, 128)

            def mixed(shift):
                return jnp.where(upper, rows(upper_k, shift), rows(lower_k, shift))

            east = pltpu.roll(rows(east_k, 0), 4, 1)
            west = pltpu.roll(rows(west_k, 0), 4, 1)
            value = (
                mixed(0) * (1.0 - 4.0 * d) + east * (d - u_c) + west * (d + u_c)
                + mixed(1) * (d - v_c) + mixed(-1) * (d + v_c)
            )
            own_rows = pl.ds(pl.multiple_of(own * SPAN + (y0 + 1) * 8, 8), 64)
            kept = second[own_rows, :].reshape(8, 8, 128)
            kept = jnp.where(upper, value, kept) if own == 1 else jnp.where(upper, kept, value)
            second[own_rows, :] = kept.reshape(64, 128)
            side_k = 0 if own == 1 else 5
            second[pl.ds(pl.multiple_of(side_k * SPAN + (y0 + 1) * 8, 8), 64), :] = value.reshape(64, 128)

    wrap(second, (1, 4))
    finish((1, 4), lambda i: late(i, 0))
    edge(0).start()
    edge(3).start()
    blocked[me] = mine[me]

    lane = lax.broadcasted_iota(jnp.int32, (256, 128), 1)
    lane_f = lane.astype(F32)
    left2 = lane < 64
    left = left2[0:128]

    lane_choice = jnp.where(left2, 0.0, 4.0)

    def picked(i, pairs):
        b = other(i)
        before, after = lax.rem(b + 15, 16), lax.rem(b + 1, 16)
        columns = []
        for group in pairs:
            pieces = []
            for kk in group:
                if 2 <= kk < 6:
                    place = PLACE[kk - 2] * 64
                    pieces.append(mine[before, place + 32:place + 64, :])
                    pieces.append(mine[b, place:place + 64, :])
                    pieces.append(mine[after, place:place + 32, :])
                else:
                    k = kk + 2 if kk < 2 else kk - 6
                    pieces.append(region[k, before, 32:64, :])
                    pieces.append(region[k, b, :, :])
                    pieces.append(region[k, after, 0:32, :])
            columns.append(jnp.concatenate(pieces, axis=0))
        return nn(hot[i], jnp.concatenate(columns, axis=1))

    for i in range(16):
        here = jnp.broadcast_to(index[:, i:i + 1], (256, 128))
        hot[i, :, 0:128] = jnp.where(here == lane_f, 1.0, 0.0).astype(BF16)
        hot[i, :, 128:256] = jnp.where(here == lane_f + 128.0, 1.0, 0.0).astype(BF16)
        values = picked(i, ((2, 3), (4, 5)))
        wanted = choice[:, i:i + 1] - lane_choice
        seen[i] = jnp.where(wanted == 0.0, values[:, 0:128], jnp.where(wanted == 1.0, values[:, 128:256], 0.0))
    for k in (1, 2, 0, 3):
        edge(k).wait()
    for i in range(16):
        values = picked(i, ((0, 7), (1, 6)))
        wanted = choice[:, i:i + 1] - lane_choice
        values = jnp.where(wanted == 2.0, values[:, 0:128], jnp.where(wanted == 3.0, values[:, 128:256], seen[i]))
        values = values + pltpu.roll(values, 64, 1)
        packed = jnp.where(left, values[0:128], values[128:256]).astype(BF16)
        if i < 15:
            seen_out[other(i)] = packed
        else:
            measured[me] = packed
        if i > 0:
            seen_copy(i - 1).start()

    @pl.loop(0, 15)
    def _(i):
        late(i, 1).start()

    def centred(start, count):
        rows = slice(start, start + count)
        left_rows = left2[rows]
        total = blocked[0, rows, :].astype(F32)
        for g in range(1, 16):
            total = total + blocked[g, rows, :].astype(F32)
        centre0 = jnp.sum(jnp.where(left_rows, total, 0.0), axis=1, keepdims=True) * (1.0 / MEMBERS)
        centre1 = jnp.sum(jnp.where(left_rows, 0.0, total), axis=1, keepdims=True) * (1.0 / MEMBERS)
        centre = jnp.where(left_rows, centre0, centre1)
        target = (start // 128) * 256 + start % 128
        for q in range(8):
            even = blocked[other(2 * q), rows, :].astype(F32) - centre
            odd = blocked[other(2 * q + 1), rows, :].astype(F32) - centre
            lanes = slice(q * 128, (q + 1) * 128)
            dev[target:target + count, lanes] = jnp.where(left_rows, even, pltpu.roll(odd, 64, 1)).astype(BF16)
            dev[target + 128:target + 128 + count, lanes] = jnp.where(
                left_rows, pltpu.roll(even, 64, 1), odd
            ).astype(BF16)
        return centre0, centre1

    @pl.loop(0, 15)
    def _(i):
        state(i).wait()

    centre_a = centred(0, 128)

    @pl.loop(0, 15)
    def _(i):
        late(i, 0).wait()

    centre_b = centred(128, 64)

    @pl.loop(0, 15)
    def _(i):
        seen_copy(i).wait()

    total = measured[0].astype(F32)
    for g in range(1, 16):
        total = total + measured[g].astype(F32)
    mean0 = jnp.sum(jnp.where(left, total, 0.0), axis=1, keepdims=True) * (1.0 / MEMBERS)
    mean1 = jnp.sum(jnp.where(left, 0.0, total), axis=1, keepdims=True) * (1.0 / MEMBERS)
    misfit = jnp.concatenate(
        [
            root_rows[part] * (value_ref[part:part + 1, :] - jnp.broadcast_to(mean, (128, 128)).T[0:16])
            for part, mean in enumerate((mean0, mean1))
        ],
        axis=1,
    )
    mean = jnp.where(left, mean0, mean1)
    root = jnp.where(left, roots[0], roots[1])
    for q in range(8):
        even = (measured[other(2 * q)].astype(F32) - mean) * root
        odd = (measured[other(2 * q + 1)].astype(F32) - mean) * root
        lanes = slice(q * 128, (q + 1) * 128)
        basis[0:128, lanes] = jnp.where(left, even, pltpu.roll(odd, 64, 1)).astype(BF16)
        basis[128:256, lanes] = jnp.where(left, pltpu.roll(even, 64, 1), odd).astype(BF16)
    small = nt(basis[...], basis[...])
    eye = lax.broadcasted_iota(jnp.int32, (256, 256), 0) == lax.broadcasted_iota(jnp.int32, (256, 256), 1)
    trace = jnp.sum(jnp.where(eye, small, 0.0), axis=(0, 1), keepdims=True)
    s = (MEMBERS - 1.0) + trace * (1.0 / MEMBERS)
    inv_s = 1.0 / s
    inv_root_s = lax.rsqrt(s)
    a = (MEMBERS - 1.0) * inv_s
    p = 1.5 - 0.5 * a
    r0 = 1.5 * p - 0.5 * a * p * p * p
    r1 = -0.75 - 0.5 * p * p * p + 0.75 * a * p * p
    r2 = 0.5 * (1.5 * p * p - 0.75 * a * p)
    r3 = (1.0 / 6.0) * (0.375 * a - 2.25 * p)
    r4 = 1.5 / 24.0
    spread = jnp.sqrt(jnp.full((1, 1), MEMBERS - 1.0, F32))
    keep = r0 * spread * inv_root_s
    g1 = small * inv_s
    g1_s = split(g1)
    g2 = nn3(g1_s, g1_s)
    g2_s = split(g2)
    g3 = nn3(g2_s, g1_s)
    g4 = nn3(g2_s, g2_s)
    mix = (jnp.where(eye, r1, 0.0) + r2 * g1 + r3 * g2 + r4 * g3) * (spread * inv_s * inv_root_s)
    step_s = split((jnp.where(eye, r0, 0.0) + r1 * g1 + r2 * g2 + r3 * g3 + r4 * g4) * inv_root_s)
    gain = nn3(split(nn3(split(misfit), step_s)), step_s)[0:1]
    mix_s = split(mix)

    def answer(part, centre):
        here = slice(part * 256, part * 256 + 256)
        rows = slice(part * 128, part * 128 + 128)
        cross = nt(dev[here, :], basis[...])
        update = nn3(split(cross), mix_s).astype(BF16)
        offset = centre + jnp.sum(cross * gain, axis=1, keepdims=True)
        for double in range(4):
            lanes = slice(double * 256, double * 256 + 256)
            both = offset + keep * dev[here, lanes].astype(F32) + nn(update, basis[:, lanes])
            for q in (2 * double, 2 * double + 1):
                value = both[:, 0:128] if q % 2 == 0 else both[:, 128:256]
                var0, var1 = value[0:128], value[128:256]
                sending[other(2 * q), rows, :] = jnp.where(left, var0, pltpu.roll(var1, 64, 1)).astype(BF16)
                odd = jnp.where(left, pltpu.roll(var0, 64, 1), var1).astype(BF16)
                if q < 7:
                    sending[other(2 * q + 1), rows, :] = odd
                else:
                    returned[me, rows, :] = odd
                if q > 0:
                    back(2 * q - 2, 2 * part).start()
                    back(2 * q - 1, 2 * part).start()
        back(14, 2 * part).start()

        @pl.loop(0, 15)
        def _(i):
            back(i, 2 * part + 1).start()

    answer(0, jnp.concatenate(centre_a, axis=0))

    @pl.loop(0, 15)
    def _(i):
        late(i, 1).wait()

    centre_c = centred(192, 64)
    answer(1, jnp.concatenate([centre_b[0], centre_c[0], centre_b[1], centre_c[1]], axis=0))

    for place in range(4):
        @pl.loop(0, 15)
        def _(i):
            back(i, place).wait()

        turn_out(returned, first, second, place)
    out_ref[...] = second[0:4096, :].astype(BF16)


def call_whole(x, d, u, v, cell, weight, value, count):
    dma = pltpu.SemaphoreType.DMA
    return pl.pallas_call(
        whole,
        out_shape=jax.ShapeDtypeStruct((4096, 128), BF16),
        in_specs=[ANY] * 7 + [pl.BlockSpec(memory_space=pltpu.SMEM)],
        out_specs=VMEM,
        scratch_shapes=[
            pltpu.VMEM((4, 128), F32),
            pltpu.SMEM((4,), F32),
            pltpu.SMEM((4,), F32),
            pltpu.VMEM((16, 256), jnp.int32),
            pltpu.VMEM((2, 128), F32),
            pltpu.VMEM((2, 128), F32),
            dma((6,)),
            pltpu.VMEM((4096, 128), F32),
            pltpu.VMEM((6 * SPAN, 128), F32),
            pltpu.VMEM((6 * SPAN, 128), F32),
            pltpu.VMEM((1024, 128), F32),
            pltpu.VMEM((2, 128, 256), F32),
            pltpu.VMEM((16, 256, 256), BF16),
            pltpu.VMEM((2, 1024, 128), BF16),
            pltpu.VMEM((2, 1024, 128), BF16),
            pltpu.VMEM((16, 256, 128), BF16),
            pltpu.VMEM((16, 256, 128), BF16),
            pltpu.VMEM((4, 16, 64, 128), BF16),
            pltpu.VMEM((16, 256, 128), F32),
            pltpu.VMEM((16, 128, 128), BF16),
            pltpu.VMEM((16, 128, 128), BF16),
            pltpu.VMEM((512, 1024), BF16),
            pltpu.VMEM((256, 1024), BF16),
            pltpu.VMEM((16, 256, 128), BF16),
            pltpu.VMEM((16, 256, 128), BF16),
            dma((4,)), dma((2,)), dma((2,)), dma((15,)), dma((15,)), dma((2, 15)), dma((2, 15)), dma((4,)), dma((4,)),
            dma((15,)), dma((15,)), dma((4, 15)), dma((4, 15)),
        ],
        compiler_params=pltpu.CompilerParams(
            vmem_limit_bytes=48000000, collective_id=0, has_side_effects=True
        ),
        name="whole",
    )(x, d, u, v, cell, weight, value, count)


def hbm(x):
    return pltpu.with_memory_space_constraint(x, pltpu.MemorySpace.HBM)


def on_device(
    starting_realizations,
    diffusivity,
    eastward_velocity,
    northward_velocity,
    obs_cell,
    obs_count,
    obs_value,
    obs_weight,
):
    analysis = call_whole(
        hbm(starting_realizations.reshape(4096, 128)), hbm(diffusivity), hbm(eastward_velocity), hbm(northward_velocity),
        hbm(obs_cell[0]), hbm(obs_weight.reshape(2, 128)), hbm(obs_value.reshape(2, 128)), obs_count,
    )
    return analysis.reshape(64, 2, 4, 8, 128)


def solution(mesh):
    return jax.shard_map(
        on_device,
        mesh=mesh,
        in_specs=(
            P("grp", None, None, "tile", None),
            P(),
            P(),
            P(),
            P("tile", None, None),
            P("tile", "grp"),
            P("tile", "grp", None),
            P("tile", "grp", None),
        ),
        out_specs=P("grp", None, None, "tile", None),
        check_vma=False,
    )
```

time: 62.6 us -> 52.3 us (0.84); the launches traced: 62.3 us -> 51.3 us
  Pallas kernels: 56.3 us -> 49.7 us
  other arithmetic: 3.16 us -> 0 us
  local copies, waits for them, and re-layouts: 2.13 us -> 0.97 us
    pallas_call x3 -> x1, Pallas kernels: 56.3 us -> 49.7 us  [call_whole(): pl.pallas_call(whole, out_shape=jax.ShapeDtypeStruct((4096, 128), BF16),...]
    concatenate x3 -> x0, other arithmetic: 2.39 us -> none  [the longest x1 0.81 us: coefficients(): jnp.concatenate([eastward_velocity] * 2)[:, None]]
    transpose x1 -> x0, other arithmetic: 0.76 us -> none  [coefficients(): jnp.concatenate([diffusivity, diffusivity], 0).T[:, :, None]]
    unnamed x7 -> x1, local copies, waits for them, and re-layouts: 1.7 us -> 0.97 us
where the time goes in v2:
time: 52.3 us; the launch traced here: 51.3 us
  Pallas kernels  49.7 us (95%)
  local copies, waits for them, and re-layouts  0.97 us (2%)
  between operations  0.66 us (1%)
    pallas_call x1, Pallas kernels, call_whole(): pl.pallas_call(whole, out_shape=jax.ShapeDtypeStruct((4096, 128), BF16),...  49.7 us

profile of v2, /device:TPU:97, one launch (start us, length us, event | category | flops | bytes accessed | tf_op | source)
XLA Modules:
  0.0 51.3 jit_solution(1988019176663647121)
XLA Ops:
  0.7 49.7 %whole.1 = bf16[4096,128]{1,0:T(8,128)(2,1)S(1)} custom-call(f32[4096,128]{1,0:T(8,128)} %bitcast.6, f32[4,128]{1,0:T(4,128)} %d_hbm.1, f32[4]{0:T(128)} %u_hbm.1, f32[4]{0:T(128)} %v_hbm.1, s32[16,256]{1,0:T(8,128)} %bitcast.7, f32[2,128]{1,0:T(2,128)} %bitcast.8, f32[2,128]{1,0:T(2,128)} %bitcast.9, s32[1,1]{1,0:T(1,128)S(6)} %copy.10.count_ref), custom_call_target="tpu_custom_call" | custom-call | tf_op jit(solution)/shard_map/whole/pallas_call | solution.py:480
  50.4 1.0 %copy.11 = bf16[64,2,4,8,128]{4,3,2,1,0:T(8,128)(2,1)} copy(bf16[64,2,4,8,128]{4,3,2,1,0:T(8,128)(2,1)S(1)} %bitcast.5) | data formatting | bytes 2097152

commit v3 on v2

--- a/solution.py
+++ b/solution.py
@@ -94,7 +94,7 @@
     d_ref, u_ref, v_ref, cell_ref, weight_ref, value_ref, small_sem, x_ref, first, second, spread_d, cells, hot, halo_out, halo_in, mine, blocked, region, seen, seen_out, measured,
     dev, basis, sending, returned,
     load_sem, halo_send, halo_recv, state_send, state_recv, late_send, late_recv, region_send, region_recv,
-    ob_send, ob_recv, back_send, back_recv,
+    strip_send, strip_recv, ob_send, ob_recv, back_send, back_recv,
 ):
     me = lax.axis_index("grp")
     tile = lax.axis_index("tile")
@@ -153,6 +153,13 @@
         return remote(
             mine.at[:, pl.ds(PLACE[k] * 64, 64)], region.at[k], region_send.at[k], region_recv.at[k],
             (me, above if k > 1 else below),
+        )
+
+    def late_edge(j, k):
+        block = lax.rem(me + j, 16)
+        return remote(
+            mine.at[block, pl.ds(PLACE[k] * 64, 64)], region.at[k, block], strip_send.at[k // 3, j],
+            strip_recv.at[k // 3, j], (me, above if k > 1 else below),
         )
 
     def seen_copy(i):
@@ -193,26 +200,11 @@
     def coef(y0):
         return spread_d[pl.ds(pl.multiple_of(y0 * 8, 64), 64), :].reshape(8, 8, 128), u[None], v[None]
 
-    def finish(k_list, send, before=None):
-        def one(b):
-            y0 = b * 8
-            for k, value in zip(k_list, stencil(second, k_list, 0, 5, y0, coef(y0), upper)):
-                place = PLACE[k - 1] * 64
-                mine[b, place:place + 64, :] = value.reshape(64, 128).astype(BF16)
-
-        one(other(0))
-
-        @pl.loop(1, 14)
-        def _(i):
-            if before is not None:
-                before(i + 2)
-            one(other(i))
-            send(i - 1).start()
-
-        one(other(14))
-        send(13).start()
-        one(me)
-        send(14).start()
+    def finish(k_list, block):
+        y0 = block * 8
+        for k, value in zip(k_list, stencil(second, k_list, 0, 5, y0, coef(y0), upper)):
+            place = PLACE[k - 1] * 64
+            mine[block, place:place + 64, :] = value.reshape(64, 128).astype(BF16)
 
     def inner(ahead):
         block = lax.rem(me + ahead, 16)
@@ -234,7 +226,18 @@
     def _(ahead):
         inner(ahead)
 
-    finish((2, 3), state, inner)
+    finish((2, 3), other(0))
+
+    @pl.loop(1, 14)
+    def _(i):
+        inner(i + 2)
+        finish((2, 3), other(i))
+        state(i - 1).start()
+
+    finish((2, 3), other(14))
+    state(13).start()
+    finish((2, 3), me)
+    state(14).start()
     edge(1).start()
     edge(2).start()
 
@@ -290,9 +293,21 @@
             second[pl.ds(pl.multiple_of(side_k * SPAN + (y0 + 1) * 8, 8), 64), :] = value.reshape(64, 128)
 
     wrap(second, (1, 4))
-    finish((1, 4), lambda i: late(i, 0))
-    edge(0).start()
-    edge(3).start()
+    finish((1, 4), me)
+    finish((1, 4), other(0))
+    late_edge(0, 0).start()
+    late_edge(0, 3).start()
+
+    @pl.loop(2, 16)
+    def _(j):
+        finish((1, 4), lax.rem(me + j, 16))
+        late_edge(j - 1, 0).start()
+        late_edge(j - 1, 3).start()
+        late(j - 2, 0).start()
+
+    late_edge(15, 0).start()
+    late_edge(15, 3).start()
+    late(14, 0).start()
     blocked[me] = mine[me]
 
     lane = lax.broadcasted_iota(jnp.int32, (256, 128), 1)
@@ -329,9 +344,13 @@
         values = picked(i, ((2, 3), (4, 5)))
         wanted = choice[:, i:i + 1] - lane_choice
         seen[i] = jnp.where(wanted == 0.0, values[:, 0:128], jnp.where(wanted == 1.0, values[:, 128:256], 0.0))
-    for k in (1, 2, 0, 3):
-        edge(k).wait()
+    edge(1).wait()
+    edge(2).wait()
     for i in range(16):
+        for j in (0, 1, 2) if i == 0 else (i + 2,):
+            if j < 16:
+                late_edge(j, 0).wait()
+                late_edge(j, 3).wait()
         values = picked(i, ((0, 7), (1, 6)))
         wanted = choice[:, i:i + 1] - lane_choice
         values = jnp.where(wanted == 2.0, values[:, 0:128], jnp.where(wanted == 3.0, values[:, 128:256], seen[i]))
@@ -391,7 +410,7 @@
     mean1 = jnp.sum(jnp.where(left, 0.0, total), axis=1, keepdims=True) * (1.0 / MEMBERS)
     misfit = jnp.concatenate(
         [
-            root_rows[part] * (value_ref[part:part + 1, :] - jnp.broadcast_to(mean, (128, 128)).T[0:16])
+            root_rows[part] * (value_ref[part:part + 1, :] - jnp.broadcast_to(mean, (128, 128)).T[0:1])
             for part, mean in enumerate((mean0, mean1))
         ],
         axis=1,
@@ -423,12 +442,14 @@
     g1_s = split(g1)
     g2 = nn3(g1_s, g1_s)
     g2_s = split(g2)
-    g3 = nn3(g2_s, g1_s)
-    g4 = nn3(g2_s, g2_s)
-    mix = (jnp.where(eye, r1, 0.0) + r2 * g1 + r3 * g2 + r4 * g3) * (spread * inv_s * inv_root_s)
-    step_s = split((jnp.where(eye, r0, 0.0) + r1 * g1 + r2 * g2 + r3 * g3 + r4 * g4) * inv_root_s)
-    gain = nn3(split(nn3(split(misfit), step_s)), step_s)[0:1]
-    mix_s = split(mix)
+    q = jnp.where(eye, r1, 0.0) + r2 * g1 + r3 * g2 + r4 * nn3(g2_s, g1_s)
+    mix_s = split(q * (spread * inv_s * inv_root_s))
+
+    def through(row):
+        column = jnp.sum(q * row, axis=1, keepdims=True)
+        return (r0 * row + jnp.sum(g1 * column, axis=0, keepdims=True)) * inv_root_s
+
+    gain = through(through(misfit))
 
     def answer(part, centre):
         here = slice(part * 256, part * 256 + 256)
@@ -509,7 +530,7 @@
             pltpu.VMEM((16, 256, 128), BF16),
             pltpu.VMEM((16, 256, 128), BF16),
             dma((4,)), dma((2,)), dma((2,)), dma((15,)), dma((15,)), dma((2, 15)), dma((2, 15)), dma((4,)), dma((4,)),
-            dma((15,)), dma((15,)), dma((4, 15)), dma((4, 15)),
+            dma((2, 16)), dma((2, 16)), dma((15,)), dma((15,)), dma((4, 15)), dma((4, 15)),
         ],
         compiler_params=pltpu.CompilerParams(
             vmem_limit_bytes=48000000, collective_id=0, has_side_effects=True

time: 52.3 us -> 49.6 us (0.948); the launches traced: 51.3 us -> 49.3 us
  Pallas kernels: 49.7 us -> 47.7 us
    pallas_call x1, Pallas kernels: 49.7 us -> 47.7 us  [call_whole(): pl.pallas_call(whole, out_shape=jax.ShapeDtypeStruct((4096, 128), BF16),...]
where the time goes in v3:
time: 49.6 us; the launch traced here: 49.3 us
  Pallas kernels  47.7 us (96%)
  local copies, waits for them, and re-layouts  0.97 us (2%)
  between operations  0.66 us (1%)
    pallas_call x1, Pallas kernels, call_whole(): pl.pallas_call(whole, out_shape=jax.ShapeDtypeStruct((4096, 128), BF16),...  47.7 us

profile of v3, /device:TPU:97, one launch (start us, length us, event | category | flops | bytes accessed | tf_op | source)
XLA Modules:
  0.0 49.3 jit_solution(868249113072028726)
XLA Ops:
  0.7 47.7 %whole.1 = bf16[4096,128]{1,0:T(8,128)(2,1)S(1)} custom-call(f32[4096,128]{1,0:T(8,128)} %bitcast.6, f32[4,128]{1,0:T(4,128)} %d_hbm.1, f32[4]{0:T(128)} %u_hbm.1, f32[4]{0:T(128)} %v_hbm.1, s32[16,256]{1,0:T(8,128)} %bitcast.7, f32[2,128]{1,0:T(2,128)} %bitcast.8, f32[2,128]{1,0:T(2,128)} %bitcast.9, s32[1,1]{1,0:T(1,128)S(6)} %copy.10.count_ref), custom_call_target="tpu_custom_call" | custom-call | tf_op jit(solution)/shard_map/whole/pallas_call | solution.py:501
  48.3 1.0 %copy.11 = bf16[64,2,4,8,128]{4,3,2,1,0:T(8,128)(2,1)} copy(bf16[64,2,4,8,128]{4,3,2,1,0:T(8,128)(2,1)S(1)} %bitcast.5) | data formatting | bytes 2097152

commit v4 on v3

--- a/solution.py
+++ b/solution.py
@@ -14,6 +14,7 @@
 ANY = pl.BlockSpec(memory_space=pl.ANY)
 PLACE = (2, 0, 1, 3)
 PAIR = (1, 2, 0, 3)
+FAR = (10, 6, 9, 14, 11, 2, 8, 5, 15, 7, 13, 1, 4, 3, 12, 0)
 SPAN = 130 * 8
 
 
@@ -165,21 +166,15 @@
     def seen_copy(i):
         return remote(seen_out.at[other(i)], measured.at[me], ob_send.at[i], ob_recv.at[i], (other(i), tile))
 
-    def back(i, place):
-        rows = pl.ds(place * 64, 64)
+    def toward(i):
+        return lax.rem(me // 4 + FAR[i] // 4, 4) * 4 + lax.rem(me + FAR[i] % 4, 4)
+
+    def back(i, part):
+        rows = pl.ds(part * 128, 128)
         return remote(
-            sending.at[other(i), rows], returned.at[me, rows], back_send.at[place, i], back_recv.at[place, i],
-            (other(i), tile),
-        )
-
-    for load in loads:
-        load.wait()
-    turn_in(x_ref, first, (0, 1, 6, 7))
-    halo_out[1] = first[SPAN + 8:SPAN + 1032, :].astype(BF16)
-    halo_out[0] = first[4 * SPAN + 8:4 * SPAN + 1032, :].astype(BF16)
-    pl.semaphore_wait(barrier, 17)
-    halo(0).start()
-    halo(1).start()
+            sending.at[toward(i), rows], returned.at[me, rows], back_send.at[part, i], back_recv.at[part, i],
+            (toward(i), tile),
+        )
 
     for load in small_loads:
         load.wait()
@@ -193,6 +188,16 @@
         here = lax.rem(sub, 4) == level
         u = jnp.where(here, 0.5 * u_ref[level], u)
         v = jnp.where(here, 0.5 * v_ref[level], v)
+
+    for load in loads:
+        load.wait()
+    turn_in(x_ref, first, (0, 1, 6, 7))
+    halo_out[1] = first[SPAN + 8:SPAN + 1032, :].astype(BF16)
+    halo_out[0] = first[4 * SPAN + 8:4 * SPAN + 1032, :].astype(BF16)
+    pl.semaphore_wait(barrier, 17)
+    halo(0).start()
+    halo(1).start()
+
     turn_in(x_ref, first, (2, 3, 4, 5))
     wrap(first, (1, 2, 3, 4))
     upper = lax.broadcasted_iota(jnp.int32, (8, 8, 128), 1) < 4
@@ -378,8 +383,8 @@
         centre = jnp.where(left_rows, centre0, centre1)
         target = (start // 128) * 256 + start % 128
         for q in range(8):
-            even = blocked[other(2 * q), rows, :].astype(F32) - centre
-            odd = blocked[other(2 * q + 1), rows, :].astype(F32) - centre
+            even = blocked[toward(2 * q), rows, :].astype(F32) - centre
+            odd = blocked[toward(2 * q + 1), rows, :].astype(F32) - centre
             lanes = slice(q * 128, (q + 1) * 128)
             dev[target:target + count, lanes] = jnp.where(left_rows, even, pltpu.roll(odd, 64, 1)).astype(BF16)
             dev[target + 128:target + 128 + count, lanes] = jnp.where(
@@ -418,8 +423,8 @@
     mean = jnp.where(left, mean0, mean1)
     root = jnp.where(left, roots[0], roots[1])
     for q in range(8):
-        even = (measured[other(2 * q)].astype(F32) - mean) * root
-        odd = (measured[other(2 * q + 1)].astype(F32) - mean) * root
+        even = (measured[toward(2 * q)].astype(F32) - mean) * root
+        odd = (measured[toward(2 * q + 1)].astype(F32) - mean) * root
         lanes = slice(q * 128, (q + 1) * 128)
         basis[0:128, lanes] = jnp.where(left, even, pltpu.roll(odd, 64, 1)).astype(BF16)
         basis[128:256, lanes] = jnp.where(left, pltpu.roll(even, 64, 1), odd).astype(BF16)
@@ -463,20 +468,16 @@
             for q in (2 * double, 2 * double + 1):
                 value = both[:, 0:128] if q % 2 == 0 else both[:, 128:256]
                 var0, var1 = value[0:128], value[128:256]
-                sending[other(2 * q), rows, :] = jnp.where(left, var0, pltpu.roll(var1, 64, 1)).astype(BF16)
+                sending[toward(2 * q), rows, :] = jnp.where(left, var0, pltpu.roll(var1, 64, 1)).astype(BF16)
                 odd = jnp.where(left, pltpu.roll(var0, 64, 1), var1).astype(BF16)
                 if q < 7:
-                    sending[other(2 * q + 1), rows, :] = odd
+                    sending[toward(2 * q + 1), rows, :] = odd
                 else:
                     returned[me, rows, :] = odd
                 if q > 0:
-                    back(2 * q - 2, 2 * part).start()
-                    back(2 * q - 1, 2 * part).start()
-        back(14, 2 * part).start()
-
-        @pl.loop(0, 15)
-        def _(i):
-            back(i, 2 * part + 1).start()
+                    back(2 * q - 2, part).start()
+                    back(2 * q - 1, part).start()
+        back(14, part).start()
 
     answer(0, jnp.concatenate(centre_a, axis=0))
 
@@ -487,12 +488,12 @@
     centre_c = centred(192, 64)
     answer(1, jnp.concatenate([centre_b[0], centre_c[0], centre_b[1], centre_c[1]], axis=0))
 
-    for place in range(4):
-        @pl.loop(0, 15)
-        def _(i):
-            back(i, place).wait()
-
-        turn_out(returned, first, second, place)
+    for part in range(2):
+        for i in range(15):
+            back(i, part).wait()
+
+        turn_out(returned, first, second, 2 * part)
+        turn_out(returned, first, second, 2 * part + 1)
     out_ref[...] = second[0:4096, :].astype(BF16)
 
 
@@ -530,7 +531,7 @@
             pltpu.VMEM((16, 256, 128), BF16),
             pltpu.VMEM((16, 256, 128), BF16),
             dma((4,)), dma((2,)), dma((2,)), dma((15,)), dma((15,)), dma((2, 15)), dma((2, 15)), dma((4,)), dma((4,)),
-            dma((2, 16)), dma((2, 16)), dma((15,)), dma((15,)), dma((4, 15)), dma((4, 15)),
+            dma((2, 16)), dma((2, 16)), dma((15,)), dma((15,)), dma((2, 15)), dma((2, 15)),
         ],
         compiler_params=pltpu.CompilerParams(
             vmem_limit_bytes=48000000, collective_id=0, has_side_effects=True

time: 49.6 us -> 49.6 us (level)
  no operation moved by 1% of the time
where the time goes in v4:
time: 49.6 us; the launch traced here: 49.2 us
  Pallas kernels  47.6 us (96%)
  local copies, waits for them, and re-layouts  0.97 us (2%)
  between operations  0.66 us (1%)
    pallas_call x1, Pallas kernels, call_whole(): pl.pallas_call(whole, out_shape=jax.ShapeDtypeStruct((4096, 128), BF16),...  47.6 us

profile of v4, /device:TPU:97, one launch (start us, length us, event | category | flops | bytes accessed | tf_op | source)
XLA Modules:
  0.0 49.2 jit_solution(15283069710583650721)
XLA Ops:
  0.7 47.6 %whole.1 = bf16[4096,128]{1,0:T(8,128)(2,1)S(1)} custom-call(f32[4096,128]{1,0:T(8,128)} %bitcast.6, f32[4,128]{1,0:T(4,128)} %d_hbm.1, f32[4]{0:T(128)} %u_hbm.1, f32[4]{0:T(128)} %v_hbm.1, s32[16,256]{1,0:T(8,128)} %bitcast.7, f32[2,128]{1,0:T(2,128)} %bitcast.8, f32[2,128]{1,0:T(2,128)} %bitcast.9, s32[1,1]{1,0:T(1,128)S(6)} %copy.10.count_ref), custom_call_target="tpu_custom_call" | custom-call | tf_op jit(solution)/shard_map/whole/pallas_call | solution.py:502
  48.2 1.0 %copy.11 = bf16[64,2,4,8,128]{4,3,2,1,0:T(8,128)(2,1)} copy(bf16[64,2,4,8,128]{4,3,2,1,0:T(8,128)(2,1)S(1)} %bitcast.5) | data formatting | bytes 2097152
